TPU v7x, 32 devices: a whole 2x2x4 slice. The times are simulated.
32 devices in a mesh: curve: 32 (over z, y, x, core).
Axes of the slice: x: 2, y: 2, z: 4, core: 2. Of those that a mesh axis runs over, the one named last changes fastest.
Arguments:
- multipole: bfloat16 [152, 32768], P(None, 'curve'), may hold values from -6 to 6
- upward_maps: bfloat16 [8, 152, 152], replicated, may hold values from -0.15625 to 0.15625
- transfer_maps: bfloat16 [316, 152, 152], replicated, may hold values from -0.03125 to 0.03125
- downward_maps: bfloat16 [8, 152, 152], replicated, may hold values from -0.5 to 0.5
- check_inverse: bfloat16 [152, 152], replicated, may hold values from -0.5 to 0.5
- fine_lists: int32 [316, 32768], P(None, 'curve'), may hold values from -1 to 1023, as said below
- coarse_lists: int32 [316, 4096], P(None, 'curve'), may hold values from -1 to 127, as said below
Outputs:
- local_density: bfloat16 [152, 32768], P(None, 'curve')
Inputs may be any that keep to these rules, and one draw needn't show every extreme that they name: `fine_lists`: entry k of box t is -1 or the place, within its own brick, of the fine box at offset k from t; it is a place only where that box lies in the grid, its parent touches the parent of t, and both boxes are present in the tree. `coarse_lists`: entry k of box t is -1 or the place, within its own brick, of the coarse box at offset k from t; it is a place only where that box lies in the grid, its parent touches the parent of t, and both boxes are present in the tree (a coarse box is present when one of its children is).
All inputs are finite; a program needn't handle non-finite values.
Results may differ from a plain program's by a relative error of at most 0.0055.
Values may be sent and summed in bfloat16 or wider, within the bound.
No kernel may reach another device: no remote copies, remote signals or barrier semaphores. Data moves between devices by JAX's collectives and lax.ppermute only.
A program may use at most 704 MiB of HBM per device.

v0:
```python
import jax
import jax.numpy as jnp
from jax import lax
from jax.sharding import PartitionSpec as P

BX = 8
BY = 8
BZ = 16


SHIFTS = [
    (first_axis, second_axis, third_axis)
    for first_axis in range(-3, 4)
    for second_axis in range(-3, 4)
    for third_axis in range(-3, 4)
    if max(abs(first_axis), abs(second_axis), abs(third_axis)) >= 2
]


def passed_along(shard, axis, by):
    devices = lax.axis_size(axis)
    return lax.ppermute(shard, axis, [(i, (i + by) % devices) for i in range(devices)])


def grid_counts(levels):
    return (2 ** (levels // 3), 2 ** ((levels + 1) // 3), 2 ** ((levels + 2) // 3))


def decode(position, levels):
    coords = [jnp.int32(0), jnp.int32(0), jnp.int32(0)]
    for bit_place in range(levels):
        weight = position // 2**bit_place % 2
        coords[2 - bit_place % 3] = coords[2 - bit_place % 3] + weight * 2 ** (bit_place // 3)
    return coords


def encode(coords, levels):
    encoded = jnp.int32(0)
    for bit_place in range(levels):
        encoded = encoded + coords[2 - bit_place % 3] // 2 ** (bit_place // 3) % 2 * 2**bit_place
    return encoded


def curve_steps(levels, axis_number):
    places = [bit_place for bit_place in range(levels) if 2 - bit_place % 3 == axis_number]

    def spread_bits(value):
        return sum(((value >> rank & 1) << place for rank, place in enumerate(places)))

    return [spread_bits(2**carry) - spread_bits(2**carry - 1) for carry in range(len(places))]


def extend_axis(density, axis_number, levels, anchor, position, mover, depth):
    devices = 2**levels
    limits = grid_counts(levels)
    extent = density.shape[1 + axis_number]
    lower_layers = lax.slice_in_dim(density, 0, depth, axis=1 + axis_number)
    upper_layers = lax.slice_in_dim(density, extent - depth, extent, axis=1 + axis_number)
    steps = curve_steps(levels, axis_number)
    received = []
    for facing in (-1, 1):
        sent = upper_layers if facing < 0 else lower_layers
        moved = [anchor[number] + (facing if number == axis_number else 0) for number in range(3)]
        inside = (moved[axis_number] >= 0) & (moved[axis_number] < limits[axis_number])
        wanted = jnp.mod(position - encode(moved, levels), devices)
        collected = jnp.zeros_like(sent)
        for step_size in steps:
            distance = step_size % devices if facing < 0 else -step_size % devices
            arrived = mover(sent, distance)
            collected = jnp.where(inside & (wanted == distance), arrived, collected)
        received.append(collected)
    return jnp.concatenate([received[0], density, received[1]], axis=1 + axis_number)


def fine_mover(slab, distance):
    return passed_along(slab, "curve", distance)


def coarse_mover(slab, distance):
    return passed_along(slab, "curve", distance)


def extend_all(density, levels, anchor, position, mover, depth):
    extended = density
    for axis_number in range(3):
        extended = extend_axis(extended, axis_number, levels, anchor, position, mover, depth)
    return extended


def upward(grid, upward_maps):
    channels, size_x, size_y, size_z = grid.shape
    children = (
        grid.reshape(channels, size_x // 2, 2, size_y // 2, 2, size_z // 2, 2)
        .transpose(2, 4, 6, 0, 1, 3, 5)
        .reshape(8, channels, -1)
    )
    parents = jnp.einsum(
        "opq,oqc->pc", upward_maps, children, preferred_element_type=jnp.float32
    ).astype(jnp.bfloat16)
    return parents.reshape(channels, size_x // 2, size_y // 2, size_z // 2)


def translate(extended, lists, operators, extent):
    channels = extended.shape[0]
    running = jnp.zeros((channels, extent[0] * extent[1] * extent[2]), jnp.float32)
    stride = (len(SHIFTS) + 3) // 4
    for start_at in range(0, len(SHIFTS), stride):
        chosen = SHIFTS[start_at : start_at + stride]
        stacked = jnp.stack(
            [
                extended[
                    :,
                    3 + offset[0] : 3 + offset[0] + extent[0],
                    3 + offset[1] : 3 + offset[1] + extent[1],
                    3 + offset[2] : 3 + offset[2] + extent[2],
                ].reshape(channels, -1)
                for offset in chosen
            ]
        )
        present = (lists[start_at : start_at + len(chosen)] >= 0).astype(stacked.dtype)
        stacked = stacked * present[:, None, :]
        running = running + jnp.einsum(
            "kpq,kqb->pb",
            operators[start_at : start_at + len(chosen)],
            stacked,
            preferred_element_type=jnp.float32,
        )
    return running


def local(
    multipole, upward_maps, transfer_maps, downward_maps, check_inverse, fine_lists, coarse_lists
):
    channels = multipole.shape[0]
    devices = lax.axis_size("curve")
    levels = devices.bit_length() - 1
    position = lax.axis_index("curve")
    anchor = decode(position, levels)
    fine_shape = (BX, BY, BZ)
    coarse_shape = (BX // 2, BY // 2, BZ // 2)
    fine_grid = multipole.reshape(channels, BX, BY, BZ)
    fine_extended = extend_all(fine_grid, levels, anchor, position, fine_mover, 3)
    parent_grid = upward(fine_grid, upward_maps)
    coarse_extended = extend_all(parent_grid, levels, anchor, position, coarse_mover, 3)
    coarse_check = 0.5 * translate(coarse_extended, coarse_lists, transfer_maps, coarse_shape)
    coarse_local = coarse_check.astype(jnp.bfloat16)
    fine_check = translate(fine_extended, fine_lists, transfer_maps, fine_shape)
    spread = jnp.einsum(
        "opq,qc->opc", downward_maps, coarse_local, preferred_element_type=jnp.float32
    )
    spread = (
        spread.reshape(2, 2, 2, channels, BX // 2, BY // 2, BZ // 2)
        .transpose(3, 4, 0, 5, 1, 6, 2)
        .reshape(channels, -1)
    )
    fine_total = (fine_check + spread).astype(jnp.bfloat16)
    return jnp.dot(check_inverse, fine_total, preferred_element_type=jnp.float32).astype(
        jnp.bfloat16
    )


def solution(mesh):
    placed = (P(None, "curve"), P(), P(), P(), P(), P(None, "curve"), P(None, "curve"))
    return jax.shard_map(
        local, mesh=mesh, in_specs=placed, out_specs=P(None, "curve"), check_vma=False
    )
```

profile of v0, /device:TPU:24, one launch (start us, length us, event | category | flops | bytes accessed | tf_op | source)
XLA Modules:
  0.0 683.3 jit_solution(16127372051678545165)
XLA Ops:
  0.0 1.2 copy.9
  1.6 1.4 fusion.82
  3.2 1.5 collective-permute-start.11
  5.9 2.3 collective-permute-start.1
  8.2 1.9 collective-permute-start
  10.2 22.0 %fusion.102 = (bf16[79,152,152]{0,2,1:T(8,128)(2,1)}, bf16[79,152,152]{0,2,1:T(8,128)(2,1)}, bf16[79,152,152]{0,2,1:T(8,128)(2,1)}, bf16[79,152,152]{0,2,1:T(8,128)(2,1)}) fusion(bf16[316,152,152]{0,2,1:T(8,128)(2,1)} %param.9), kind=kLoop, calls=%fused_computation.745 | loop fusion | bytes 29203456 | tf_op jit(solution)/shard_map/slice | solution.py:124
  33.8 14.8 %copy.16 = bf16[79,152,152]{1,2,0:T(8,128)(2,1)} copy(bf16[79,152,152]{0,2,1:T(8,128)(2,1)} %get-tuple-element.7) | data formatting | bytes 7300864 | tf_op jit(solution)/shard_map/slice | solution.py:124
  48.6 14.7 %copy.17 = bf16[79,152,152]{1,2,0:T(8,128)(2,1)} copy(bf16[79,152,152]{0,2,1:T(8,128)(2,1)} %get-tuple-element.6) | data formatting | bytes 7300864 | tf_op jit(solution)/shard_map/slice | solution.py:124
  63.4 14.7 %copy.18 = bf16[79,152,152]{1,2,0:T(8,128)(2,1)} copy(bf16[79,152,152]{0,2,1:T(8,128)(2,1)} %get-tuple-element.8) | data formatting | bytes 7300864 | tf_op jit(solution)/shard_map/slice | solution.py:124
  78.1 14.8 %copy.19 = bf16[79,152,152]{1,2,0:T(8,128)(2,1)} copy(bf16[79,152,152]{0,2,1:T(8,128)(2,1)} %get-tuple-element.5) | data formatting | bytes 7300864 | tf_op jit(solution)/shard_map/slice | solution.py:124
  93.0 2.0 collective-permute-start.15
  95.0 3.8 collective-permute-start.12
  98.8 3.5 collective-permute-done.14
  102.3 2.7 collective-permute-start.13
  105.1 3.5 collective-permute-done.12
  109.3 4.4 collective-permute-start.19
  114.1 1.6 collective-permute-start.17
  116.8 1.4 pad_maximum_fusion.3
  118.3 4.6 collective-permute-start.5
  122.9 1.7 collective-permute-start.2
  124.7 1.2 collective-permute-done.16
  133.0 1.2 copy-done.284
  135.3 1.2 copy-done.282
  137.6 1.5 copy-done.280
  139.1 2.6 copy-done.2
  142.2 7.4 %fusion.55 = f32[128,152]{0,1:T(8,128)S(1)} fusion(bf16[79,152,152]{1,2,0:T(8,128)(2,1)S(1)} %bitcast.734, bf16[79,152,128]{1,2,0:T(8,128)(2,1)} %copy-done.284, bf16[79,128]{1,0:T(8,128)(2,1)S(1)} %copy-done.279), kind=kOutput, calls=%fused_computation.673 | convolution fusion | flops 468792320 | bytes 6822528 | tf_op jit(solution)/shard_map/kpq,kqb->pb/dot_general | solution.py:122
  149.7 4.2 fusion.76
  154.0 4.1 fusion.73
  158.1 8.7 %convolution_bitcast_fusion = f32[8,152,128]{2,1,0:T(8,128)S(1)} fusion(bf16[8,152,152]{2,1,0:T(8,128)(2,1)S(1)} %copy-done, f32[128,152]{0,1:T(8,128)S(1)} %fusion.73, bf16[79,152,152]{1,2,0:T(8,128)(2,1)} %copy.19, bf16[79,152,128]{1,2,0:T(8,128)(2,1)} %copy-done.2, bf16[79,128]{1,0:T(8,128)(2,1)S(1)} %copy-done.275), kind=kOutput, calls=%fused_computation.670 | convolution fusion | flops 516167680 | bytes 7814784 | tf_op jit(solution)/shard_map/opq,qc->opc/dot_general | solution.py:148
  167.1 1.8 copy.15
  168.9 2.9 reshape.27
  174.3 1.8 collective-permute-start.8
  176.1 5.6 collective-permute-start.9
  181.7 2.3 collective-permute-start.6
  184.0 3.5 collective-permute-start.7
  188.0 3.7 fusion.119
  191.7 3.7 fusion.120
  195.7 3.9 collective-permute-done.6
  199.6 1.3 collective-permute-done.7
  201.1 4.3 pad_maximum_fusion
  205.4 5.6 fusion.115
  211.0 5.7 fusion.114
  216.7 4.3 fusion.113
  221.0 4.1 fusion.112
  225.1 5.7 fusion.111
  230.8 3.9 fusion.118
  234.7 3.9 fusion.117
  238.6 4.7 fusion.116
  243.3 4.7 fusion.110
  248.0 5.8 fusion.109
  253.8 4.4 fusion.108
  258.2 5.4 fusion.107
  263.6 3.7 fusion.106
  267.3 4.3 fusion.105
  271.5 1.1 fusion.104
  272.7 1.4 fusion.103
  274.9 2.1 constant_dynamic-update-slice_fusion.78
  277.1 1.9 constant_dynamic-update-slice_fusion.236
  279.0 1.9 constant_dynamic-update-slice_fusion.315
  347.0 38.1 %fusion.30 = f32[1024,152]{1,0:T(8,128)} fusion(bf16[79,152,152]{1,2,0:T(8,128)(2,1)S(1)} %bitcast.744, bf16[79,152,1024]{1,2,0:T(8,128)(2,1)} %constant_dynamic-update-slice_fusion.79, bf16[79,1024]{1,0:T(8,128)(2,1)S(1)} %copy-done.274), kind=kOutput, calls=%fused_computation.28 | convolution fusion | flops 3750338560 | bytes 29027200 | tf_op jit(solution)/shard_map/kpq,kqb->pb/dot_general | solution.py:122
  583.1 34.8 %fusion.27 = f32[1024,152]{1,0:T(8,128)S(1)} fusion(f32[1024,152]{1,0:T(8,128)S(1)} %copy-done.285, bf16[79,152,152]{1,2,0:T(8,128)(2,1)S(1)} %bitcast.736, bf16[79,152,1024]{1,2,0:T(8,128)(2,1)} %constant_dynamic-update-slice_fusion, bf16[79,1024]{1,0:T(8,128)(2,1)S(1)} %copy-done.273), kind=kOutput, calls=%fused_computation.27 | convolution fusion | flops 3750494208 | bytes 29649792 | tf_op jit(solution)/shard_map/kpq,kqb->pb/dot_general | solution.py:122
  618.0 37.0 %fusion.36 = f32[1024,152]{1,0:T(8,128)S(1)} fusion(f32[1024,152]{1,0:T(8,128)S(1)} %fusion.27, bf16[79,152,152]{1,2,0:T(8,128)(2,1)S(1)} %bitcast.740, bf16[79,152,1024]{1,2,0:T(8,128)(2,1)} %constant_dynamic-update-slice_fusion.158, bf16[79,1024]{1,0:T(8,128)(2,1)S(1)} %copy-done.272), kind=kOutput, calls=%fused_computation.30 | convolution fusion | flops 3750494208 | bytes 29649792 | tf_op jit(solution)/shard_map/kpq,kqb->pb/dot_general | solution.py:122
  655.1 26.7 %fusion.51 = bf16[152,1024]{0,1:T(8,128)(2,1)S(1)} fusion(f32[152,1024]{0,1:T(8,128)S(1)} %copy-done.269, f32[1024,152]{1,0:T(8,128)S(1)} %fusion.36, bf16[79,152,152]{1,2,0:T(8,128)(2,1)S(1)} %bitcast.732, bf16[79,152,1024]{1,2,0:T(8,128)(2,1)} %constant_dynamic-update-slice_fusion.237, bf16[79,1024]{1,0:T(8,128)(2,1)S(1)} %copy-done.271), kind=kOutput, calls=%fused_computation.35 | convolution fusion | flops 3750805504 | bytes 29961088 | tf_op jit(solution)/shard_map/kpq,kqb->pb/dot_general | solution.py:122
  681.8 1.0 fusion.54
  (1301 shorter events, 281.3 us)
Async XLA Ops:
  0.0 158.1 %copy-start = (bf16[8,152,152]{2,1,0:T(8,128)(2,1)S(1)}, bf16[8,152,152]{2,1,0:T(8,128)(2,1)}, u32[]{:S(2)}) copy-start(bf16[8,152,152]{2,1,0:T(8,128)(2,1)} %param.10) | copy-start | bytes 1108996
  3.2 89.7 %collective-permute-start.11 = (bf16[152,3,4,8]{0,3,2,1:T(8,128)(2,1)S(1)}, bf16[152,3,4,8]{0,3,2,1:T(8,128)(2,1)S(1)}, u32[]{:S(2)}, u32[]{:S(2)}) collective-permute-start(bf16[152,3,4,8]{0,3,2,1:T(8,128)(2,1)S(1)} %get-tuple-element.672), channel_id=1, source_target_pairs={{0,28},{1,29},{2,30},{3,31},{4,0},{5,1},{6,2},{7,3},{8,4},{9,5},{1... | collective-permute-start | bytes 87560 | tf_op jit(solution)/shard_map/ppermute | solution.py:22
  4.6 88.3 %collective-permute-start.10 = (bf16[152,3,4,8]{0,3,2,1:T(8,128)(2,1)S(1)}, bf16[152,3,4,8]{0,3,2,1:T(8,128)(2,1)S(1)}, u32[]{:S(2)}, u32[]{:S(2)}) collective-permute-start(bf16[152,3,4,8]{0,3,2,1:T(8,128)(2,1)S(1)} %get-tuple-element.671), channel_id=1, source_target_pairs={{0,4},{1,5},{2,6},{3,7},{4,8},{5,9},{6,10},{7,11},{8,12},{9,13},{1... | collective-permute-start | bytes 87560 | tf_op jit(solution)/shard_map/ppermute | solution.py:22
  5.9 108.2 %collective-permute-start.1 = (bf16[152,3,8,16]{0,3,2,1:T(8,128)(2,1)S(1)}, bf16[152,3,8,16]{0,3,2,1:T(8,128)(2,1)S(1)}, u32[]{:S(2)}, u32[]{:S(2)}) collective-permute-start(bf16[152,3,8,16]{0,3,2,1:T(8,128)(2,1)S(1)} %get-tuple-element.616), channel_id=1, source_target_pairs={{0,28},{1,29},{2,30},{3,31},{4,0},{5,1},{6,2},{7,3},{8,4},{9,5},{1... | collective-permute-start | bytes 350216 | tf_op jit(solution)/shard_map/ppermute | solution.py:22
  8.2 23.9 %copy-start.268 = (s32[316,1024]{1,0:T(8,128)S(1)}, s32[316,1024]{1,0:T(8,128)}, u32[]{:S(2)}) copy-start(s32[316,1024]{1,0:T(8,128)} %param.12) | copy-start | bytes 3883012
  8.2 24.9 %copy-start.270 = (s32[316,128]{1,0:T(8,128)S(1)}, s32[316,128]{1,0:T(8,128)}, u32[]{:S(2)}) copy-start(s32[316,128]{1,0:T(8,128)} %param.13) | copy-start | bytes 485380
  8.2 107.5 %collective-permute-start = (bf16[152,3,8,16]{0,3,2,1:T(8,128)(2,1)}, bf16[152,3,8,16]{0,3,2,1:T(8,128)(2,1)S(1)}, u32[]{:S(2)}, u32[]{:S(2)}) collective-permute-start(bf16[152,3,8,16]{0,3,2,1:T(8,128)(2,1)} %get-tuple-element.615), channel_id=1, source_target_pairs={{0,4},{1,5},{2,6},{3,7},{4,8},{5,9},{6,10},{7,11},{8,12},{9,13},{1... | collective-permute-start | bytes 350216 | tf_op jit(solution)/shard_map/ppermute | solution.py:22
  93.0 9.3 %collective-permute-start.14 = (bf16[152,10,3,8]{0,3,2,1:T(8,128)(2,1)S(1)}, bf16[152,10,3,8]{0,3,2,1:T(8,128)(2,1)S(1)}, u32[]{:S(2)}, u32[]{:S(2)}) collective-permute-start(bf16[152,10,3,8]{0,3,2,1:T(8,128)(2,1)S(1)} %get-tuple-element.664), channel_id=1, source_target_pairs={{0,18},{1,19},{2,20},{3,21},{4,22},{5,23},{6,24},{7,25},{8,26},{9,... | collective-permute-start | bytes 218888 | tf_op jit(solution)/shard_map/ppermute | solution.py:22
  93.0 12.0 %collective-permute-start.15 = (bf16[152,10,3,8]{0,3,2,1:T(8,128)(2,1)S(1)}, bf16[152,10,3,8]{0,3,2,1:T(8,128)(2,1)S(1)}, u32[]{:S(2)}, u32[]{:S(2)}) collective-permute-start(bf16[152,10,3,8]{0,3,2,1:T(8,128)(2,1)S(1)} %get-tuple-element.664), channel_id=1, source_target_pairs={{0,30},{1,31},{2,0},{3,1},{4,2},{5,3},{6,4},{7,5},{8,6},{9,7},{10,... | collective-permute-start | bytes 218888 | tf_op jit(solution)/shard_map/ppermute | solution.py:22
  95.0 13.5 %collective-permute-start.12 = (bf16[152,10,3,8]{0,3,2,1:T(8,128)(2,1)S(1)}, bf16[152,10,3,8]{0,3,2,1:T(8,128)(2,1)S(1)}, u32[]{:S(2)}, u32[]{:S(2)}) collective-permute-start(bf16[152,10,3,8]{0,3,2,1:T(8,128)(2,1)S(1)} %get-tuple-element.663), channel_id=1, source_target_pairs={{0,14},{1,15},{2,16},{3,17},{4,18},{5,19},{6,20},{7,21},{8,22},{9,... | collective-permute-start | bytes 218888 | tf_op jit(solution)/shard_map/ppermute | solution.py:22
  102.3 6.7 collective-permute-start.13
  109.3 9.0 %collective-permute-start.18 = (bf16[152,10,10,3]{0,3,2,1:T(4,128)(2,1)S(1)}, bf16[152,10,10,3]{0,3,2,1:T(4,128)(2,1)S(1)}, u32[]{:S(2)}, u32[]{:S(2)}) collective-permute-start(bf16[152,10,10,3]{0,3,2,1:T(4,128)(2,1)S(1)} %get-tuple-element.619), channel_id=1, source_target_pairs={{0,25},{1,26},{2,27},{3,28},{4,29},{5,30},{6,31},{7,0},{8,1},{9,2}... | collective-permute-start | bytes 273608 | tf_op jit(solution)/shard_map/ppermute | solution.py:22
  109.3 13.6 %collective-permute-start.19 = (bf16[152,10,10,3]{0,3,2,1:T(4,128)(2,1)S(1)}, bf16[152,10,10,3]{0,3,2,1:T(4,128)(2,1)S(1)}, u32[]{:S(2)}, u32[]{:S(2)}) collective-permute-start(bf16[152,10,10,3]{0,3,2,1:T(4,128)(2,1)S(1)} %get-tuple-element.619), channel_id=1, source_target_pairs={{0,31},{1,0},{2,1},{3,2},{4,3},{5,4},{6,5},{7,6},{8,7},{9,8},{10,9... | collective-permute-start | bytes 273608 | tf_op jit(solution)/shard_map/ppermute | solution.py:22
  113.9 12.0 %collective-permute-start.16 = (bf16[152,10,10,3]{0,3,2,1:T(4,128)(2,1)S(1)}, bf16[152,10,10,3]{0,3,2,1:T(4,128)(2,1)S(1)}, u32[]{:S(2)}, u32[]{:S(2)}) collective-permute-start(bf16[152,10,10,3]{0,3,2,1:T(4,128)(2,1)S(1)} %get-tuple-element.620), channel_id=1, source_target_pairs={{0,7},{1,8},{2,9},{3,10},{4,11},{5,12},{6,13},{7,14},{8,15},{9,16}... | collective-permute-start | bytes 273608 | tf_op jit(solution)/shard_map/ppermute | solution.py:22
  114.1 12.4 %collective-permute-start.17 = (bf16[152,10,10,3]{0,3,2,1:T(4,128)(2,1)S(1)}, bf16[152,10,10,3]{0,3,2,1:T(4,128)(2,1)S(1)}, u32[]{:S(2)}, u32[]{:S(2)}) collective-permute-start(bf16[152,10,10,3]{0,3,2,1:T(4,128)(2,1)S(1)} %get-tuple-element.620), channel_id=1, source_target_pairs={{0,1},{1,2},{2,3},{3,4},{4,5},{5,6},{6,7},{7,8},{8,9},{9,10},{10,1... | collective-permute-start | bytes 273608 | tf_op jit(solution)/shard_map/ppermute | solution.py:22
  116.8 55.0 %collective-permute-start.4 = (bf16[152,14,3,16]{0,3,2,1:T(8,128)(2,1)}, bf16[152,14,3,16]{0,3,2,1:T(8,128)(2,1)S(1)}, u32[]{:S(2)}, u32[]{:S(2)}) collective-permute-start(bf16[152,14,3,16]{0,3,2,1:T(8,128)(2,1)} %get-tuple-element.332), channel_id=1, source_target_pairs={{0,18},{1,19},{2,20},{3,21},{4,22},{5,23},{6,24},{7,25},{8,26},{9,... | collective-permute-start | bytes 612872 | tf_op jit(solution)/shard_map/ppermute | solution.py:22
  118.3 53.6 %collective-permute-start.5 = (bf16[152,14,3,16]{0,3,2,1:T(8,128)(2,1)}, bf16[152,14,3,16]{0,3,2,1:T(8,128)(2,1)}, u32[]{:S(2)}, u32[]{:S(2)}) collective-permute-start(bf16[152,14,3,16]{0,3,2,1:T(8,128)(2,1)} %get-tuple-element.332), channel_id=1, source_target_pairs={{0,30},{1,31},{2,0},{3,1},{4,2},{5,3},{6,4},{7,5},{8,6},{9,7},{10,... | collective-permute-start | bytes 612872 | tf_op jit(solution)/shard_map/ppermute | solution.py:22
  122.9 50.0 %collective-permute-start.2 = (bf16[152,14,3,16]{0,3,2,1:T(8,128)(2,1)}, bf16[152,14,3,16]{0,3,2,1:T(8,128)(2,1)}, u32[]{:S(2)}, u32[]{:S(2)}) collective-permute-start(bf16[152,14,3,16]{0,3,2,1:T(8,128)(2,1)} %get-tuple-element.331), channel_id=1, source_target_pairs={{0,14},{1,15},{2,16},{3,17},{4,18},{5,19},{6,20},{7,21},{8,22},{9,... | collective-permute-start | bytes 612872 | tf_op jit(solution)/shard_map/ppermute | solution.py:22
  125.9 47.0 %collective-permute-start.3 = (bf16[152,14,3,16]{0,3,2,1:T(8,128)(2,1)}, bf16[152,14,3,16]{0,3,2,1:T(8,128)(2,1)}, u32[]{:S(2)}, u32[]{:S(2)}) collective-permute-start(bf16[152,14,3,16]{0,3,2,1:T(8,128)(2,1)} %get-tuple-element.331), channel_id=1, source_target_pairs={{0,2},{1,3},{2,4},{3,5},{4,6},{5,7},{6,8},{7,9},{8,10},{9,11},{10,... | collective-permute-start | bytes 612872 | tf_op jit(solution)/shard_map/ppermute | solution.py:22
  137.3 12.2 %slice-start.10 = ((s8[6148096]{0:T(1024)(128)(4,1)}), s8[4194304]{0:T(1024)(128)(4,1)S(1)}, s32[]{:S(2)}) async-start(s8[6148096]{0:T(1024)(128)(4,1)} %bitcast.741), calls=%async_computation.10 | async-start | bytes 8388608
  142.2 11.7 %slice-start.6 = ((s8[6148096]{0:T(1024)(128)(4,1)}), s8[1953792]{0:T(1024)(128)(4,1)S(1)}, s32[]{:S(2)}) async-start(s8[6148096]{0:T(1024)(128)(4,1)} %bitcast.737), calls=%async_computation.6 | async-start | bytes 3907584
  174.3 21.1 %collective-permute-start.8 = (bf16[152,14,14,3]{0,3,2,1:T(4,128)(2,1)S(1)}, bf16[152,14,14,3]{0,3,2,1:T(4,128)(2,1)S(1)}, u32[]{:S(2)}, u32[]{:S(2)}) collective-permute-start(bf16[152,14,14,3]{0,3,2,1:T(4,128)(2,1)S(1)} %get-tuple-element.287), channel_id=1, source_target_pairs={{0,25},{1,26},{2,27},{3,28},{4,29},{5,30},{6,31},{7,0},{8,1},{9,2}... | collective-permute-start | bytes 536264 | tf_op jit(solution)/shard_map/ppermute | solution.py:22
  176.1 19.4 %collective-permute-start.9 = (bf16[152,14,14,3]{0,3,2,1:T(4,128)(2,1)S(1)}, bf16[152,14,14,3]{0,3,2,1:T(4,128)(2,1)S(1)}, u32[]{:S(2)}, u32[]{:S(2)}) collective-permute-start(bf16[152,14,14,3]{0,3,2,1:T(4,128)(2,1)S(1)} %get-tuple-element.287), channel_id=1, source_target_pairs={{0,31},{1,0},{2,1},{3,2},{4,3},{5,4},{6,5},{7,6},{8,7},{9,8},{10,9... | collective-permute-start | bytes 536264 | tf_op jit(solution)/shard_map/ppermute | solution.py:22
  181.7 17.9 %collective-permute-start.6 = (bf16[152,14,14,3]{0,3,2,1:T(4,128)(2,1)S(1)}, bf16[152,14,14,3]{0,3,2,1:T(4,128)(2,1)S(1)}, u32[]{:S(2)}, u32[]{:S(2)}) collective-permute-start(bf16[152,14,14,3]{0,3,2,1:T(4,128)(2,1)S(1)} %get-tuple-element.288), channel_id=1, source_target_pairs={{0,7},{1,8},{2,9},{3,10},{4,11},{5,12},{6,13},{7,14},{8,15},{9,16}... | collective-permute-start | bytes 536264 | tf_op jit(solution)/shard_map/ppermute | solution.py:22
  184.0 16.9 %collective-permute-start.7 = (bf16[152,14,14,3]{0,3,2,1:T(4,128)(2,1)S(1)}, bf16[152,14,14,3]{0,3,2,1:T(4,128)(2,1)S(1)}, u32[]{:S(2)}, u32[]{:S(2)}) collective-permute-start(bf16[152,14,14,3]{0,3,2,1:T(4,128)(2,1)S(1)} %get-tuple-element.288), channel_id=1, source_target_pairs={{0,1},{1,2},{2,3},{3,4},{4,5},{5,6},{6,7},{7,8},{8,9},{9,10},{10,1... | collective-permute-start | bytes 536264 | tf_op jit(solution)/shard_map/ppermute | solution.py:22
  274.1 8.6 %copy-start.260 = (bf16[152,8,8,16]{0,3,2,1:T(8,128)(2,1)S(1)}, bf16[152,8,8,16]{0,3,2,1:T(8,128)(2,1)}, u32[]{:S(2)}) copy-start(bf16[152,8,8,16]{0,3,2,1:T(8,128)(2,1)} %get-tuple-element.218) | copy-start | bytes 933892
  274.1 9.4 %copy-start.258 = (bf16[152,8,8,16]{0,3,2,1:T(8,128)(2,1)S(1)}, bf16[152,8,8,16]{0,3,2,1:T(8,128)(2,1)}, u32[]{:S(2)}) copy-start(bf16[152,8,8,16]{0,3,2,1:T(8,128)(2,1)} %get-tuple-element.217) | copy-start | bytes 933892
  274.1 10.3 %copy-start.263 = (bf16[152,8,8,16]{0,3,2,1:T(8,128)(2,1)S(1)}, bf16[152,8,8,16]{0,3,2,1:T(8,128)(2,1)}, u32[]{:S(2)}) copy-start(bf16[152,8,8,16]{0,3,2,1:T(8,128)(2,1)} %get-tuple-element.197) | copy-start | bytes 933892
  274.1 11.1 %copy-start.262 = (bf16[152,8,8,16]{0,3,2,1:T(8,128)(2,1)S(1)}, bf16[152,8,8,16]{0,3,2,1:T(8,128)(2,1)}, u32[]{:S(2)}) copy-start(bf16[152,8,8,16]{0,3,2,1:T(8,128)(2,1)} %get-tuple-element.196) | copy-start | bytes 933892
  274.1 11.9 %copy-start.261 = (bf16[152,8,8,16]{0,3,2,1:T(8,128)(2,1)S(1)}, bf16[152,8,8,16]{0,3,2,1:T(8,128)(2,1)}, u32[]{:S(2)}) copy-start(bf16[152,8,8,16]{0,3,2,1:T(8,128)(2,1)} %get-tuple-element.195) | copy-start | bytes 933892
  274.9 11.9 %copy-start.211 = (bf16[152,8,8,16]{0,3,2,1:T(8,128)(2,1)S(1)}, bf16[152,8,8,16]{0,3,2,1:T(8,128)(2,1)}, u32[]{:S(2)}) copy-start(bf16[152,8,8,16]{0,3,2,1:T(8,128)(2,1)} %get-tuple-element.306) | copy-start | bytes 933892
  277.1 10.6 %copy-start.255 = (bf16[152,8,8,16]{0,3,2,1:T(8,128)(2,1)S(1)}, bf16[152,8,8,16]{0,3,2,1:T(8,128)(2,1)}, u32[]{:S(2)}) copy-start(bf16[152,8,8,16]{0,3,2,1:T(8,128)(2,1)} %get-tuple-element.216) | copy-start | bytes 933892
  279.0 9.5 %copy-start.253 = (bf16[152,8,8,16]{0,3,2,1:T(8,128)(2,1)S(1)}, bf16[152,8,8,16]{0,3,2,1:T(8,128)(2,1)}, u32[]{:S(2)}) copy-start(bf16[152,8,8,16]{0,3,2,1:T(8,128)(2,1)} %get-tuple-element.215) | copy-start | bytes 933892
  299.5 8.6 %copy-start.240 = (bf16[152,8,8,16]{0,3,2,1:T(8,128)(2,1)S(1)}, bf16[152,8,8,16]{0,3,2,1:T(8,128)(2,1)}, u32[]{:S(2)}) copy-start(bf16[152,8,8,16]{0,3,2,1:T(8,128)(2,1)} %get-tuple-element.185) | copy-start | bytes 933892
  319.8 8.6 %copy-start.217 = (bf16[152,8,8,16]{0,3,2,1:T(8,128)(2,1)S(1)}, bf16[152,8,8,16]{0,3,2,1:T(8,128)(2,1)}, u32[]{:S(2)}) copy-start(bf16[152,8,8,16]{0,3,2,1:T(8,128)(2,1)} %get-tuple-element.155) | copy-start | bytes 933892
  320.7 8.6 %copy-start.215 = (bf16[152,8,8,16]{0,3,2,1:T(8,128)(2,1)S(1)}, bf16[152,8,8,16]{0,3,2,1:T(8,128)(2,1)}, u32[]{:S(2)}) copy-start(bf16[152,8,8,16]{0,3,2,1:T(8,128)(2,1)} %get-tuple-element.154) | copy-start | bytes 933892
  322.4 8.6 %copy-start.206 = (bf16[152,8,8,16]{0,3,2,1:T(8,128)(2,1)S(1)}, bf16[152,8,8,16]{0,3,2,1:T(8,128)(2,1)}, u32[]{:S(2)}) copy-start(bf16[152,8,8,16]{0,3,2,1:T(8,128)(2,1)} %get-tuple-element.171) | copy-start | bytes 933892
  326.6 8.6 %copy-start.208 = (bf16[152,8,8,16]{0,3,2,1:T(8,128)(2,1)S(1)}, bf16[152,8,8,16]{0,3,2,1:T(8,128)(2,1)}, u32[]{:S(2)}) copy-start(bf16[152,8,8,16]{0,3,2,1:T(8,128)(2,1)} %get-tuple-element.151) | copy-start | bytes 933892
  334.3 12.6 %slice-start.12 = ((s8[6148096]{0:T(1024)(128)(4,1)}), s8[4194304]{0:T(1024)(128)(4,1)S(1)}, s32[]{:S(2)}) async-start(s8[6148096]{0:T(1024)(128)(4,1)} %bitcast.743), calls=%async_computation.12 | async-start | bytes 8388608
  347.0 38.2 %copy-start.191 = (bf16[152,8,8,16]{0,3,2,1:T(8,128)(2,1)S(1)}, bf16[152,8,8,16]{0,3,2,1:T(8,128)(2,1)}, u32[]{:S(2)}) copy-start(bf16[152,8,8,16]{0,3,2,1:T(8,128)(2,1)} %get-tuple-element.283) | copy-start | bytes 933892
  347.0 39.0 %copy-start.189 = (bf16[152,8,8,16]{0,3,2,1:T(8,128)(2,1)S(1)}, bf16[152,8,8,16]{0,3,2,1:T(8,128)(2,1)}, u32[]{:S(2)}) copy-start(bf16[152,8,8,16]{0,3,2,1:T(8,128)(2,1)} %get-tuple-element.282) | copy-start | bytes 933892
  347.0 39.9 %copy-start.142 = (bf16[152,8,8,16]{0,3,2,1:T(8,128)(2,1)S(1)}, bf16[152,8,8,16]{0,3,2,1:T(8,128)(2,1)}, u32[]{:S(2)}) copy-start(bf16[152,8,8,16]{0,3,2,1:T(8,128)(2,1)} %get-tuple-element.328) | copy-start | bytes 933892
  347.0 40.7 %copy-start.194 = (bf16[152,8,8,16]{0,3,2,1:T(8,128)(2,1)S(1)}, bf16[152,8,8,16]{0,3,2,1:T(8,128)(2,1)}, u32[]{:S(2)}) copy-start(bf16[152,8,8,16]{0,3,2,1:T(8,128)(2,1)} %get-tuple-element.270) | copy-start | bytes 933892
  347.0 41.5 %copy-start.193 = (bf16[152,8,8,16]{0,3,2,1:T(8,128)(2,1)S(1)}, bf16[152,8,8,16]{0,3,2,1:T(8,128)(2,1)}, u32[]{:S(2)}) copy-start(bf16[152,8,8,16]{0,3,2,1:T(8,128)(2,1)} %get-tuple-element.269) | copy-start | bytes 933892
  389.4 8.6 %copy-start.173 = (bf16[152,8,8,16]{0,3,2,1:T(8,128)(2,1)S(1)}, bf16[152,8,8,16]{0,3,2,1:T(8,128)(2,1)}, u32[]{:S(2)}) copy-start(bf16[152,8,8,16]{0,3,2,1:T(8,128)(2,1)} %get-tuple-element.276) | copy-start | bytes 933892
  390.2 8.6 %copy-start.135 = (bf16[152,8,8,16]{0,3,2,1:T(8,128)(2,1)S(1)}, bf16[152,8,8,16]{0,3,2,1:T(8,128)(2,1)}, u32[]{:S(2)}) copy-start(bf16[152,8,8,16]{0,3,2,1:T(8,128)(2,1)} %get-tuple-element.326) | copy-start | bytes 933892
  392.8 8.6 %copy-start.175 = (bf16[152,8,8,16]{0,3,2,1:T(8,128)(2,1)S(1)}, bf16[152,8,8,16]{0,3,2,1:T(8,128)(2,1)}, u32[]{:S(2)}) copy-start(bf16[152,8,8,16]{0,3,2,1:T(8,128)(2,1)} %get-tuple-element.262) | copy-start | bytes 933892
  494.9 8.6 %copy-start.15 = (bf16[152,8,8,16]{0,3,2,1:T(8,128)(2,1)S(1)}, bf16[152,8,8,16]{0,3,2,1:T(8,128)(2,1)}, u32[]{:S(2)}) copy-start(bf16[152,8,8,16]{0,3,2,1:T(8,128)(2,1)} %get-tuple-element.316) | copy-start | bytes 933892
  495.8 8.6 %copy-start.58 = (bf16[152,8,8,16]{0,3,2,1:T(8,128)(2,1)S(1)}, bf16[152,8,8,16]{0,3,2,1:T(8,128)(2,1)}, u32[]{:S(2)}) copy-start(bf16[152,8,8,16]{0,3,2,1:T(8,128)(2,1)} %get-tuple-element.79) | copy-start | bytes 933892
  497.4 8.6 %copy-start.56 = (bf16[152,8,8,16]{0,3,2,1:T(8,128)(2,1)S(1)}, bf16[152,8,8,16]{0,3,2,1:T(8,128)(2,1)}, u32[]{:S(2)}) copy-start(bf16[152,8,8,16]{0,3,2,1:T(8,128)(2,1)} %get-tuple-element.77) | copy-start | bytes 933892
  498.3 8.6 %copy-start.48 = (bf16[152,8,8,16]{0,3,2,1:T(8,128)(2,1)S(1)}, bf16[152,8,8,16]{0,3,2,1:T(8,128)(2,1)}, u32[]{:S(2)}) copy-start(bf16[152,8,8,16]{0,3,2,1:T(8,128)(2,1)} %get-tuple-element.95) | copy-start | bytes 933892
  516.1 8.6 %copy-start.34 = (bf16[152,8,8,16]{0,3,2,1:T(8,128)(2,1)S(1)}, bf16[152,8,8,16]{0,3,2,1:T(8,128)(2,1)}, u32[]{:S(2)}) copy-start(bf16[152,8,8,16]{0,3,2,1:T(8,128)(2,1)} %get-tuple-element.66) | copy-start | bytes 933892
  518.6 8.6 %copy-start.27 = (bf16[152,8,8,16]{0,3,2,1:T(8,128)(2,1)S(1)}, bf16[152,8,8,16]{0,3,2,1:T(8,128)(2,1)}, u32[]{:S(2)}) copy-start(bf16[152,8,8,16]{0,3,2,1:T(8,128)(2,1)} %get-tuple-element.67) | copy-start | bytes 933892
  519.5 8.6 %copy-start.38 = (bf16[152,8,8,16]{0,3,2,1:T(8,128)(2,1)S(1)}, bf16[152,8,8,16]{0,3,2,1:T(8,128)(2,1)}, u32[]{:S(2)}) copy-start(bf16[152,8,8,16]{0,3,2,1:T(8,128)(2,1)} %get-tuple-element.47) | copy-start | bytes 933892
  570.2 12.6 %slice-start.4 = ((s8[6148096]{0:T(1024)(128)(4,1)}), s8[4194304]{0:T(1024)(128)(4,1)S(1)}, s32[]{:S(2)}) async-start(s8[6148096]{0:T(1024)(128)(4,1)} %bitcast.735), calls=%async_computation.4 | async-start | bytes 8388608
  577.8 40.2 %slice-start.8 = ((s8[6148096]{0:T(1024)(128)(4,1)}), s8[4194304]{0:T(1024)(128)(4,1)S(1)}, s32[]{:S(2)}) async-start(s8[6148096]{0:T(1024)(128)(4,1)} %bitcast.739), calls=%async_computation.8 | async-start | bytes 8388608
  583.1 34.9 %slice-start.9 = ((s8[6148096]{0:T(1024)(128)(4,1)}), s8[1953792]{0:T(1024)(128)(4,1)S(1)}, s32[]{:S(2)}) async-start(s8[6148096]{0:T(1024)(128)(4,1)} %bitcast.739), calls=%async_computation.9 | async-start | bytes 3907584
  583.1 34.9 %copy-start.272 = (bf16[79,1024]{1,0:T(8,128)(2,1)S(1)}, bf16[79,1024]{1,0:T(8,128)(2,1)}, u32[]{:S(2)}) copy-start(bf16[79,1024]{1,0:T(8,128)(2,1)} %get-tuple-element.292) | copy-start | bytes 485380
  583.1 71.9 %slice-start = ((s8[6148096]{0:T(1024)(128)(4,1)}), s8[4194304]{0:T(1024)(128)(4,1)S(1)}, s32[]{:S(2)}) async-start(s8[6148096]{0:T(1024)(128)(4,1)} %bitcast.731), calls=%async_computation | async-start | bytes 8388608
  618.0 37.1 %slice-start.1 = ((s8[6148096]{0:T(1024)(128)(4,1)}), s8[1953792]{0:T(1024)(128)(4,1)S(1)}, s32[]{:S(2)}) async-start(s8[6148096]{0:T(1024)(128)(4,1)} %bitcast.731), calls=%async_computation.1 | async-start | bytes 3907584
  618.0 37.0 %copy-start.269 = (f32[152,1024]{0,1:T(8,128)S(1)}, f32[152,1024]{0,1:T(8,128)}, u32[]{:S(2)}) copy-start(f32[152,1024]{0,1:T(8,128)} %reshape.27) | copy-start | bytes 1867780
  618.0 37.0 %copy-start.271 = (bf16[79,1024]{1,0:T(8,128)(2,1)S(1)}, bf16[79,1024]{1,0:T(8,128)(2,1)}, u32[]{:S(2)}) copy-start(bf16[79,1024]{1,0:T(8,128)(2,1)} %get-tuple-element.289) | copy-start | bytes 485380
  655.1 26.7 %copy-start.276 = (bf16[152,152]{1,0:T(8,128)(2,1)S(1)}, bf16[152,152]{1,0:T(8,128)(2,1)}, u32[]{:S(2)}) copy-start(bf16[152,152]{1,0:T(8,128)(2,1)} %param.11) | copy-start | bytes 138628
  655.1 27.8 %copy-start.1 = (bf16[8,152,152]{2,1,0:T(8,128)(2,1)S(1)}, bf16[8,152,152]{2,1,0:T(8,128)(2,1)}, u32[]{:S(2)}) copy-start(bf16[8,152,152]{2,1,0:T(8,128)(2,1)} %param.10) | copy-start | bytes 1108996
  (256 other events, 2095.4 us)
where the time goes:
time: 697 us; the launch traced here: 683 us
  local copies, waits for them, and re-layouts  448 us (64%)
  matrix products  163 us (23%)
  starting transfers between devices  41.1 us (6%)
  waiting for transfers between devices  13.9 us (2%)
  other arithmetic  13 us (2%)
    unnamed x1225, local copies, waits for them, and re-layouts  277 us
    dot_general x7, matrix products, translate(): jnp.einsum('kpq,kqb->pb', operators[start_at:start_at + len(chosen)], sta...  152 us
    slice x5, local copies, waits for them, and re-layouts, translate(): operators[start_at:start_at + len(chosen)]  81.1 us
    slice x36, local copies, waits for them, and re-layouts, translate(): extended[:, 3 + offset[0]:3 + offset[0] + extent[0], 3 + offset[1]:3 + of...  79.4 us
    ppermute x20, starting transfers between devices, passed_along(): lax.ppermute(shard, axis, [(i, (i + by) % devices) for i in range(devices)])  41.1 us
  transfers between devices with their start and end apart: 20, of which 6 were waited for; matrix products, arithmetic and copies ran while one was open for 19% of the time, Pallas kernels for 0%

commit v1 on v0

v1 whole, which is shorter than its diff:
```python
import itertools

import jax
import jax.numpy as jnp
import numpy as np
from jax import lax
from jax.experimental import pallas as pl
from jax.experimental.pallas import tpu as pltpu
from jax.sharding import PartitionSpec as P

BX, BY, BZ = 8, 8, 16
PX, PY, PZ = BX // 2, BY // 2, BZ // 2
LANES = PX * PY * PZ
EXT = (PX, PY, PZ)
BF = jnp.bfloat16
F32 = jnp.float32
SHIFTS = [
    d for d in itertools.product(range(-3, 4), repeat=3) if max(abs(d[0]), abs(d[1]), abs(d[2])) >= 2
]
NUMBER = {d: n for n, d in enumerate(SHIFTS)}
MIB = 1 << 20


def grid_counts(levels):
    return (2 ** (levels // 3), 2 ** ((levels + 1) // 3), 2 ** ((levels + 2) // 3))


def decode(position, levels):
    coords = [0, 0, 0]
    for bit_place in range(levels):
        coords[2 - bit_place % 3] += (position >> bit_place & 1) << (bit_place // 3)
    return coords


def encode(coords, levels):
    number = 0
    for bit_place in range(levels):
        number += (coords[2 - bit_place % 3] >> (bit_place // 3) & 1) << bit_place
    return number


def swap_pairs(devices, levels, axis, odd):
    pairs = []
    for number in range(devices):
        coords = decode(number, levels)
        if coords[axis] % 2 == odd and coords[axis] + 1 < grid_counts(levels)[axis]:
            coords[axis] += 1
            other = encode(coords, levels)
            pairs += [(number, other), (other, number)]
    return pairs


def lane_of(e):
    return (e[0] * PY * PZ + e[1] * PZ + e[2]) % LANES


def coords_of(axis, outside, depth):
    if outside:
        return list(range(-depth, 0)) + list(range(EXT[axis], EXT[axis] + depth))
    return list(range(EXT[axis]))


def elements(kind, depth):
    return itertools.product(*[coords_of(axis, kind[axis], depth) for axis in range(3)])


class Masks:
    def __init__(self):
        self.rows = {}
        self.table = []

    def add(self, name, lanes):
        row = np.zeros(LANES, np.float32)
        row[sorted(lanes)] = 1
        self.rows[name] = len(self.table)
        self.table.append(row)


KINDS_YZ = [(0, 0, 0), (0, 1, 0), (0, 0, 1), (0, 1, 1)]
ALL_KINDS = [tuple(k) for k in itertools.product((0, 1), repeat=3)]


def build_masks():
    masks = Masks()
    every = range(LANES)
    for depth in (1, 2):
        reach = 1 if depth == 1 else 3
        for kind in ALL_KINDS:
            for axis in range(3):
                if kind[axis]:
                    masks.add(
                        ("plus", depth, kind, axis),
                        {lane_of(e) for e in elements(kind, depth) if e[axis] >= EXT[axis]},
                    )
        for axis in range(3):
            kinds = {0: KINDS_YZ, 1: [(0, 0, 0), (0, 0, 1)], 2: [(0, 0, 0)]}[axis]
            for kind in kinds:
                for step in range(-reach, reach + 1):
                    lanes = set()
                    for e in elements(kind, depth):
                        moved = list(e)
                        moved[axis] += step
                        if not 0 <= moved[axis] < EXT[axis]:
                            lanes.add(lane_of(moved))
                    masks.add(("stage", depth, axis, kind, step), lanes)
    for s in range(8):
        masks.add(("zpack", s), {l for l in every if l % PZ == s})
    row = PY * PZ
    low_z = {lane_of((i, 0, k)) for i in range(PX) for k in (-1, PZ)}
    up_z = {lane_of((i, PY - 1, k)) for i in range(PX) for k in (-1, PZ)}
    masks.add(("ysrc", 0), low_z)
    masks.add(("ysrc", 1), up_z)
    for t in range(3):
        masks.add(("ypack", t), {l for l in every if (l % row) // 10 == t})
    masks.add(("xsrc_a", 0), set(range(row)))
    masks.add(("xsrc_a", 1), set(range(LANES - row, LANES)))
    for side, i in ((0, 0), (1, PX - 1)):
        masks.add(("xsrc_b", side), {lane_of((i, j, k)) for j in range(PY) for k in (-1, PZ)})
    for t in range(2):
        masks.add(("xpack_a", t), {l for l in every if l // 64 == t})
    for t in range(8):
        u, v = t % 4, t // 4
        masks.add(("xpack_b", t), {l for l in every if l // 64 == v and l % 8 in (2 * u, 2 * u + 1)})
    return masks


MASKS = build_masks()
TABLE = np.stack(MASKS.table)


def pick(tab, name, yes, no):
    n = MASKS.rows[name]
    row = jnp.broadcast_to(tab[n : n + 1, :], yes.shape).astype(BF)
    return jnp.where(row > 0, yes, no)


def roll(x, by):
    by = by % LANES
    return x if by == 0 else pltpu.roll(x, by, 1)


def padded(x, rows):
    return jnp.concatenate([x, jnp.zeros((rows - x.shape[0], x.shape[1]), x.dtype)], 0)


def octant_order():
    row = np.arange(PX * BY * BZ)
    i, y, z = row // (BY * BZ), row // BZ % BY, row % BZ
    column = (2 * (y % 2) + z % 2) * LANES + i * PY * PZ + (y // 2) * PZ + z // 2
    hot = np.zeros((len(row), len(row)), np.float32)
    hot[row, column] = 1
    return hot


def to_octants(x, hot):
    layer = BY * BZ
    halves = []
    for a in range(2):
        chunk = jnp.concatenate(
            [x[:, (2 * i + a) * layer : (2 * i + a + 1) * layer] for i in range(PX)], 1
        )
        halves.append(jnp.dot(chunk, hot, preferred_element_type=F32))
    return halves


def prep_kernel(par, mult, up, hot, tab, own, coarse, send_a, send_b):
    chans = mult.shape[0]
    rows = own.shape[1]
    halves = to_octants(mult[...], hot[...])
    total = jnp.zeros((chans, LANES), F32)
    pack = [None, None]
    for s in range(8):
        x = halves[s // 4][:, (s % 4) * LANES : (s % 4 + 1) * LANES].astype(BF)
        total = total + jnp.dot(up[s], x, preferred_element_type=F32)
        x = padded(x, rows)
        own[s] = x
        for side in range(2):
            moved = roll(x, s - (PZ - 1) * side)
            pack[side] = moved if s == 0 else pick(tab, ("zpack", s), moved, pack[side])
    c = padded(total.astype(BF), rows)
    coarse[...] = c
    even = par[2] == 0
    send_a[0] = jnp.where(even, pack[1], pack[0])
    send_b[0] = jnp.where(even, pack[0], pack[1])
    send_a[1] = c
    send_b[1] = c


def sides(par, axis, got_a, got_b):
    even = par[axis] == 0
    plus = jnp.where(even, got_a, got_b)
    minus = jnp.where(even, got_b, got_a)
    return plus, minus


def y_kernel(par, own, coarse, got_a, got_b, tab, hz, cz, send_a, send_b):
    p, m = sides(par, 2, got_a[0], got_b[0])
    for s in range(8):
        hz[s] = pick(
            tab, ("plus", 1, (0, 0, 1), 2), roll(p, PZ - s), roll(m, -1 - s)
        )
    p, m = sides(par, 2, got_a[1], got_b[1])
    far = pick(tab, ("plus", 2, (0, 0, 1), 2), roll(p, PZ), roll(m, -PZ))
    cz[...] = far
    even = par[1] == 0
    pack = [[None] * 3, [None] * 3]
    for s in range(8):
        block, t = s // 3, s % 3
        for side in range(2):
            src = pick(tab, ("ysrc", side), hz[s], own[s])
            moved = roll(src, 1 + 10 * t - (PY - 1) * PZ * side)
            pack[side][block] = (
                moved if t == 0 else pick(tab, ("ypack", t), moved, pack[side][block])
            )
    for block in range(3):
        send_a[block] = jnp.where(even, pack[1][block], pack[0][block])
        send_b[block] = jnp.where(even, pack[0][block], pack[1][block])
    for send in (send_a, send_b):
        send[3] = coarse[...]
        send[4] = far


def x_kernel(par, own, coarse, hz, cz, got_a, got_b, tab, hy, hyz, cy, cyz, send_a, send_b):
    row = PY * PZ
    for s in range(8):
        block, t = s // 3, s % 3
        p, m = sides(par, 1, got_a[block], got_b[block])
        p = roll(p, row - 1 - 10 * t)
        m = roll(m, -PZ - 1 - 10 * t)
        hy[s] = pick(tab, ("plus", 1, (0, 1, 0), 1), p, m)
        hyz[s] = pick(tab, ("plus", 1, (0, 1, 1), 1), p, m)
    near = []
    for n, kind in ((3, (0, 1, 0)), (4, (0, 1, 1))):
        p, m = sides(par, 1, got_a[n], got_b[n])
        near.append(pick(tab, ("plus", 2, kind, 1), roll(p, row), roll(m, -row)))
    cy[...] = near[0]
    cyz[...] = near[1]
    even = par[0] == 0
    pack_a = [[None] * 4, [None] * 4]
    pack_b = [None, None]
    for s in range(8):
        block, t = s // 2, s % 2
        u, v = s % 4, s // 4
        for side in range(2):
            a = pick(tab, ("xsrc_a", side), own[s], hy[s])
            b = pick(tab, ("xsrc_b", side), hz[s], hyz[s])
            a = roll(a, 8 + 64 * t - (PX - 1) * row * side)
            b = roll(b, 9 + 2 * u + 64 * v - (PX - 1) * row * side)
            pack_a[side][block] = a if t == 0 else pick(tab, ("xpack_a", t), a, pack_a[side][block])
            pack_b[side] = b if s == 0 else pick(tab, ("xpack_b", s), b, pack_b[side])
    for block in range(4):
        send_a[block] = jnp.where(even, pack_a[1][block], pack_a[0][block])
        send_b[block] = jnp.where(even, pack_a[0][block], pack_a[1][block])
    send_a[4] = jnp.where(even, pack_b[1], pack_b[0])
    send_b[4] = jnp.where(even, pack_b[0], pack_b[1])
    for send in (send_a, send_b):
        send[5] = coarse[...]
        send[6] = near[0]
        send[7] = cz[...]
        send[8] = near[1]


def offset_sets():
    fours = []

    def add(offsets):
        start = len(fours)
        for n in range(0, len(offsets), 4):
            fours.append(tuple(offsets[n : n + 4]))
        return list(range(start, len(fours)))

    small = range(-2, 3)
    sets = {}
    sets["free"] = add([d for d in SHIFTS if max(map(abs, d)) == 2])
    for axis in range(3):
        for sign in (-3, 3):
            sets[axis, sign] = add(
                [d for d in SHIFTS if d[axis] == sign and all(abs(d[o]) <= 2 for o in range(3) if o != axis)]
            )
    for sx in (-3, 3):
        for sy in (-3, 3):
            sets["xy", sx, sy] = add([(sx, sy, z) for z in small])
        for sz in (-3, 3):
            sets["xz", sx, sz] = add([(sx, y, sz) for y in small])
    for sy in (-3, 3):
        for sz in (-3, 3):
            sets["yz", sy, sz] = add([(x, sy, sz) for x in range(-3, 4)])
    return fours, sets


FOURS, SETS = offset_sets()
SIGN = (3, -3)


def jobs_of(j):
    one, two = j // 2, j % 2
    big = SETS["free"] + SETS[0, SIGN[one]] + SETS[1, SIGN[two]] + SETS["xy", SIGN[one], SIGN[two]]
    mid = SETS[2, SIGN[two]] + SETS["xz", SIGN[one], SIGN[two]]
    small = SETS["yz", SIGN[one], SIGN[two]]
    return [
        (big, (one, two, 0), (one, two, 1)),
        (mid, (one, 0, two), (one, 1, two)),
        (small, (0, one, two), (1, one, two)),
    ]


def slot_of(octant, d):
    place = [octant[n] + d[n] for n in range(3)]
    moved = [min(max(p // 2, -1), 1) for p in place]
    s = [p % 2 for p in place]
    return ((moved[0] + 1) * 9 + (moved[1] + 1) * 3 + moved[2] + 1) * 8 + 4 * s[0] + 2 * s[1] + s[2]


def octant_number(o):
    return 4 * o[0] + 2 * o[1] + o[2]


def fine_table():
    rows, shape = [], None
    for j in range(4):
        row, form = [], []
        for fours, first, second in jobs_of(j):
            row += [octant_number(first), octant_number(second)]
            counts = []
            for f in fours:
                row.append(f)
                counts.append(len(FOURS[f]))
                for d in FOURS[f]:
                    row += [NUMBER[d], slot_of(first, d), slot_of(second, d)]
            form.append(counts)
        assert shape is None or shape == form
        rows.append(row)
        shape = form
    return np.array(rows, np.int32), shape


FINE_TABLE, FINE_FORM = fine_table()


def coarse_table(spare):
    rows = []
    for four in FOURS:
        for n in range(4):
            d = four[n] if n < len(four) else None
            if d is None:
                rows.append((0, spare, 3 * 7 + 3, 0))
            else:
                rows.append((NUMBER[d], NUMBER[d], (d[0] + 3) * 7 + d[1] + 3, d[2] + 3))
    return np.array(rows, np.int32)


def rest_order(offsets):
    hot = np.zeros((offsets, 4 * LANES), np.float32)
    for n, four in enumerate(FOURS):
        for place, d in enumerate(four):
            hot[NUMBER[d], place * LANES + n] = 1
    return hot


def operator_kernel(w, order, main, rest):
    block, chans, offsets = w.shape
    at = pl.multiple_of(pl.program_id(0) * block, block)
    main[:, pl.ds(at, block), :] = jnp.transpose(w[:, 0:LANES, :], (2, 0, 1))
    left = chans - LANES
    stacked = []
    for n in range(block):
        y = jnp.dot(w[n, LANES:chans, :], order[...], preferred_element_type=F32).astype(BF)
        y = padded(y, 32)
        stacked.append(
            jnp.concatenate([y[:, m * LANES : (m + 1) * LANES] for m in range(4)], 0)
        )
    turned = jnp.transpose(jnp.stack(stacked), (2, 0, 1))
    rest[:, pl.ds(at, block), :] = turned[0 : rest.shape[0]]


def mask_kernel(fine, hot, out):
    keep = (fine[...] >= 0).astype(F32).astype(BF)
    halves = to_octants(keep, hot[...])
    offsets = fine.shape[0]
    for s in range(8):
        out[s, 0:offsets, :] = halves[s // 4][:, (s % 4) * LANES : (s % 4 + 1) * LANES]


def shifted(tab, depth, axis, kind, step, inside, outside):
    if step == 0:
        return inside
    stride = (PY * PZ, PZ, 1)[axis]
    return roll(pick(tab, ("stage", depth, axis, kind, step), outside, inside), -step * stride)


def dot_pieces(pieces):
    left = jnp.concatenate([p[0] for p in pieces], 1)
    right = jnp.concatenate([p[1] for p in pieces], 0)
    return jnp.dot(left, right, preferred_element_type=F32)


def main_kernel(
    par, ft, ct, own, hz, hy, hyz, coarse, cz, cy, cyz, got_a, got_b, tab, main, rest, keep, clist,
    down, inverse, hot, out, slots, acc, cacc, plane, cmask,
):
    chans = acc.shape[1]
    rows = own.shape[1]
    row = PY * PZ
    for s in range(8):
        block, t = s // 2, s % 2
        u, v = s % 4, s // 4
        p, m = sides(par, 0, got_a[block], got_b[block])
        p, m = roll(p, -8 - 64 * t), roll(m, -8 - 64 * t + (PX - 1) * row)
        hx = pick(tab, ("plus", 1, (1, 0, 0), 0), p, m)
        hxy = pick(tab, ("plus", 1, (1, 1, 0), 0), p, m)
        p, m = sides(par, 0, got_a[4], got_b[4])
        p, m = roll(p, -9 - 2 * u - 64 * v), roll(m, -9 - 2 * u - 64 * v + (PX - 1) * row)
        hxz = pick(tab, ("plus", 1, (1, 0, 1), 0), p, m)
        hxyz = pick(tab, ("plus", 1, (1, 1, 1), 0), p, m)
        inner = {(0, 0, 0): own[s], (0, 1, 0): hy[s], (0, 0, 1): hz[s], (0, 1, 1): hyz[s]}
        outer = {(0, 0, 0): hx, (0, 1, 0): hxy, (0, 0, 1): hxz, (0, 1, 1): hxyz}
        for dx in (-1, 0, 1):
            x = {k: shifted(tab, 1, 0, k, dx, inner[k], outer[k]) for k in KINDS_YZ}
            for dy in (-1, 0, 1):
                y = {
                    z: shifted(tab, 1, 1, (0, 0, z), dy, x[0, 0, z], x[0, 1, z]) for z in (0, 1)
                }
                for dz in (-1, 0, 1):
                    n = ((dx + 1) * 9 + (dy + 1) * 3 + dz + 1) * 8 + s
                    slots[n] = shifted(tab, 1, 2, (0, 0, 0), dz, y[0], y[1])
    inner = {(0, 0, 0): coarse[...], (0, 1, 0): cy[...], (0, 0, 1): cz[...], (0, 1, 1): cyz[...]}
    outer = {}
    for n, k in ((5, (0, 0, 0)), (6, (0, 1, 0)), (7, (0, 0, 1)), (8, (0, 1, 1))):
        p, m = sides(par, 0, got_a[n], got_b[n])
        outer[k] = pick(tab, ("plus", 2, (1, k[1], k[2]), 0), p, m)
    for dx in range(-3, 4):
        x = {k: shifted(tab, 2, 0, k, dx, inner[k], outer[k]) for k in KINDS_YZ}
        for dy in range(-3, 4):
            for z in (0, 1):
                plane[((dx + 3) * 7 + dy + 3) * 2 + z] = shifted(
                    tab, 2, 1, (0, 0, z), dy, x[0, 0, z], x[0, 1, z]
                )
    offsets = clist.shape[0]
    cmask[...] = jnp.zeros_like(cmask)
    cmask[0:offsets, :] = (clist[...] >= 0).astype(F32)
    acc[...] = jnp.zeros_like(acc)
    cacc[...] = jnp.zeros_like(cacc)
    first = MASKS.rows["stage", 2, 2, (0, 0, 0), -3]

    def coarse_body(it, carry):
        pieces = []
        for f in range(7):
            rests = []
            four = it * 7 + f
            for n in range(4):
                at = (four * 4 + n) * 4
                d, md, pn, dz = ct[at], ct[at + 1], ct[at + 2], ct[at + 3]
                far = jnp.broadcast_to(tab[pl.ds(first + dz, 1), :], (rows, LANES)).astype(BF)
                src = jnp.where(far > 0, plane[pn * 2 + 1], plane[pn * 2])
                src = pltpu.roll(src, LANES + 3 - dz, 1)
                mask = jnp.broadcast_to(cmask[pl.ds(md, 1), :], (rows, LANES)).astype(BF)
                x = src * mask
                pieces.append((main[d], x[0:LANES]))
                rests.append(x[LANES:rows])
            pieces.append((rest[four], jnp.concatenate(rests, 0)))
        cacc[...] += dot_pieces(pieces)
        return carry

    lax.fori_loop(0, len(FOURS) // 7, coarse_body, 0)

    def fine_body(j, carry):
        at = j * FINE_TABLE.shape[1]
        for counts in FINE_FORM:
            first_o, second_o = ft[at], ft[at + 1]
            at = at + 2
            pieces = []

            def flush(part):
                got = dot_pieces(part)
                acc[first_o] += got[:, 0:LANES]
                acc[second_o] += got[:, LANES:]

            for count in counts:
                four = ft[at]
                at = at + 1
                rests = []
                for n in range(count):
                    d, one, two = ft[at], ft[at + 1], ft[at + 2]
                    at = at + 3
                    x = []
                    for slot, o in ((one, first_o), (two, second_o)):
                        mask = jnp.broadcast_to(keep[o, pl.ds(d, 1), :], (rows, LANES)).astype(BF)
                        x.append(slots[slot] * mask)
                    x = jnp.concatenate(x, 1)
                    pieces.append((main[d], x[0:LANES]))
                    rests.append(x[LANES:rows])
                if count < 4:
                    rests.append(jnp.zeros((32 * (4 - count), 2 * LANES), BF))
                pieces.append((rest[four], jnp.concatenate(rests, 0)))
                while len(pieces) >= 20:
                    flush(pieces[:20])
                    pieces = pieces[20:]
            if pieces:
                flush(pieces)
        return carry

    lax.fori_loop(0, 4, fine_body, 0)
    local = (0.5 * cacc[...]).astype(BF)
    total = []
    for s in range(8):
        spread = jnp.dot(down[s], local, preferred_element_type=F32)
        total.append((acc[s] + spread).astype(BF))
    density = jnp.dot(inverse[...], jnp.concatenate(total, 1), preferred_element_type=F32).astype(BF)
    half = 4 * LANES
    layer = BY * BZ
    for a in range(2):
        natural = lax.dot_general(
            density[:, a * half : (a + 1) * half],
            hot[...],
            (((1,), (1,)), ((), ())),
            preferred_element_type=F32,
        ).astype(BF)
        for i in range(PX):
            out[:, (2 * i + a) * layer : (2 * i + a + 1) * layer] = natural[:, i * layer : (i + 1) * layer]


VMEM = pl.BlockSpec(memory_space=pltpu.VMEM)
SMEM = pl.BlockSpec(memory_space=pltpu.SMEM)


def call(kernel, name, smem, operands, outs, limit, scratch=(), flops=0, bytes_=0):
    shapes = [jax.ShapeDtypeStruct(s, t) for s, t in outs]
    return pl.pallas_call(
        kernel,
        name=name,
        in_specs=[SMEM] * smem + [VMEM] * (len(operands) - smem),
        out_specs=[VMEM] * len(shapes),
        out_shape=shapes,
        scratch_shapes=list(scratch),
        compiler_params=pltpu.CompilerParams(vmem_limit_bytes=limit),
        cost_estimate=pl.CostEstimate(flops=flops, bytes_accessed=bytes_, transcendentals=0),
    )(*operands)


def local(
    multipole, upward_maps, transfer_maps, downward_maps, check_inverse, fine_lists, coarse_lists
):
    chans = multipole.shape[0]
    offsets = transfer_maps.shape[0]
    rows = (chans + 31) // 32 * 32
    devices = lax.axis_size("curve")
    levels = devices.bit_length() - 1
    limits = grid_counts(levels)
    position = lax.axis_index("curve")
    par = jnp.stack([position >> (2 - axis) & 1 for axis in range(3)]).astype(jnp.int32)
    hot = jnp.asarray(octant_order(), BF)
    tab = jnp.asarray(TABLE)
    row_pad = (offsets + 8) // 8 * 8

    def exchange(axis, a, b):
        got_a = lax.ppermute(a, "curve", swap_pairs(devices, levels, axis, 0))
        pairs = swap_pairs(devices, levels, axis, 1)
        got_b = lax.ppermute(b, "curve", pairs) if pairs else jnp.zeros_like(b)
        return got_a, got_b

    full = ((8, rows, LANES), BF)
    one = ((rows, LANES), BF)
    own, coarse, a, b = call(
        prep_kernel, "prep", 1, (par, multipole, upward_maps, hot, tab),
        [full, one, ((2, rows, LANES), BF), ((2, rows, LANES), BF)], 16 * MIB,
        flops=10**9, bytes_=2 * MIB,
    )
    za, zb = exchange(2, a, b)
    hz, cz, a, b = call(
        y_kernel, "pack_y", 1, (par, own, coarse, za, zb, tab),
        [full, one, ((5, rows, LANES), BF), ((5, rows, LANES), BF)], 16 * MIB,
        flops=10**6, bytes_=2 * MIB,
    )
    ya, yb = exchange(1, a, b)
    hy, hyz, cy, cyz, a, b = call(
        x_kernel, "pack_x", 1, (par, own, coarse, hz, cz, ya, yb, tab),
        [full, full, one, one, ((9, rows, LANES), BF), ((9, rows, LANES), BF)], 16 * MIB,
        flops=10**6, bytes_=2 * MIB,
    )
    xa, xb = exchange(0, a, b)

    block = 8
    rests = (len(FOURS) + 7) // 8 * 8
    turned = jnp.transpose(transfer_maps, (1, 2, 0))
    order = jnp.asarray(rest_order(offsets), BF)
    main, rest = pl.pallas_call(
        operator_kernel,
        name="operators",
        grid=(chans // block,),
        in_specs=[
            pl.BlockSpec((block, chans, offsets), lambda n: (n, 0, 0)),
            pl.BlockSpec(order.shape, lambda n: (0, 0)),
        ],
        out_specs=[VMEM, VMEM],
        out_shape=[
            jax.ShapeDtypeStruct((offsets, chans, LANES), BF),
            jax.ShapeDtypeStruct((rests, chans, LANES), BF),
        ],
        compiler_params=pltpu.CompilerParams(vmem_limit_bytes=30 * MIB),
        cost_estimate=pl.CostEstimate(flops=10**10, bytes_accessed=18 * MIB, transcendentals=0),
    )(turned, order)
    (keep,) = call(
        mask_kernel, "masks", 0, (fine_lists, hot), [((8, row_pad, LANES), F32)], 16 * MIB,
        flops=10**9, bytes_=2 * MIB,
    )
    ft = jnp.asarray(FINE_TABLE.reshape(-1))
    ct = jnp.asarray(coarse_table(row_pad - 1).reshape(-1))
    (out,) = call(
        main_kernel, "translate", 3,
        (par, ft, ct, own, hz, hy, hyz, coarse, cz, cy, cyz, xa, xb, tab, main, rest, keep,
         coarse_lists, downward_maps, check_inverse, hot),
        [((chans, multipole.shape[1]), BF)],
        44 * MIB,
        scratch=[
            pltpu.VMEM((216, rows, LANES), BF),
            pltpu.VMEM((8, chans, LANES), F32),
            pltpu.VMEM((chans, LANES), F32),
            pltpu.VMEM((98, rows, LANES), BF),
            pltpu.VMEM((row_pad, LANES), F32),
        ],
        flops=2 * 10**10, bytes_=20 * MIB,
    )
    return out


def solution(mesh):
    placed = (P(None, "curve"), P(), P(), P(), P(), P(None, "curve"), P(None, "curve"))
    return jax.shard_map(
        local, mesh=mesh, in_specs=placed, out_specs=P(None, "curve"), check_vma=False
    )
```

time: 697 us -> 91.7 us (0.13); the launches traced: 683 us -> 91 us
  local copies, waits for them, and re-layouts: 448 us -> 8.96 us
  matrix products: 163 us -> 0 us
  Pallas kernels: 0 us -> 61.9 us
  starting transfers between devices: 41.1 us -> 7.8 us
  other arithmetic: 13 us -> 0.08 us
    unnamed x1225 -> x28, local copies, waits for them, and re-layouts: 277 us -> 8.91 us
    dot_general x10 -> x0, matrix products: 163 us -> none  [the longest x7 152 us: translate(): jnp.einsum('kpq,kqb->pb', operators[start_at:start_at + len(chosen)], sta...]
    slice x45 -> x0, local copies, waits for them, and re-layouts: 161 us -> none  [the longest x5 81.1 us: translate(): operators[start_at:start_at + len(chosen)]]
    pallas_call x0 -> x6, Pallas kernels: none -> 61.9 us  [the longest x5 42.3 us: call(): pl.pallas_call(kernel, name=name, in_specs=[SMEM] * smem + [VMEM] * (len(...]
    ppermute x20 -> x5, starting transfers between devices: 41.1 us -> 7.8 us  [the longest x2 4.65 us: exchange(): got_b = lax.ppermute(b, 'curve', pairs) if pairs else jnp.zeros_like(b)]
    concatenate x9 -> x0, other arithmetic: 7.54 us -> none  [extend_axis(): jnp.concatenate([received[0], density, received[1]], axis=1 + axis_number)]
  transfers between devices with their start and end apart: 20 -> 5, of which waited for: 6 -> 3; matrix products, arithmetic and copies ran while one was open for 19% -> 0% of each run, Pallas kernels for 0% -> 22%
where the time goes in v1:
time: 91.7 us; the launch traced here: 91 us
  Pallas kernels  61.9 us (68%)
  waiting for transfers between devices  12.1 us (13%)
  local copies, waits for them, and re-layouts  8.96 us (10%)
  starting transfers between devices  7.8 us (9%)
    pallas_call x5, Pallas kernels, call(): pl.pallas_call(kernel, name=name, in_specs=[SMEM] * smem + [VMEM] * (len(...  42.3 us
    pallas_call x1, Pallas kernels, local(): pl.pallas_call(operator_kernel, name='operators', grid=(chans // block,),...  19.6 us
    ppermute x2, waiting for transfers between devices, exchange(): got_b = lax.ppermute(b, 'curve', pairs) if pairs else jnp.zeros_like(b)  9.41 us
    unnamed x28, local copies, waits for them, and re-layouts  8.91 us
    ppermute x2, starting transfers between devices, exchange(): got_b = lax.ppermute(b, 'curve', pairs) if pairs else jnp.zeros_like(b)  4.65 us
    ppermute x3, starting transfers between devices, exchange(): got_a = lax.ppermute(a, 'curve', swap_pairs(devices, levels, axis, 0))  3.15 us
    ppermute x3, waiting for transfers between devices, exchange(): got_a = lax.ppermute(a, 'curve', swap_pairs(devices, levels, axis, 0))  2.73 us
  transfers between devices with their start and end apart: 5, of which 3 were waited for; matrix products, arithmetic and copies ran while one was open for 0% of the time, Pallas kernels for 22%

profile of v1, /device:TPU:24, one launch (start us, length us, event | category | flops | bytes accessed | tf_op | source)
XLA Modules:
  0.0 91.0 jit_solution(11991442809219125841)
XLA Ops:
  0.0 0.1 pad_add_fusion.par
  0.1 0.0 copy-start
  0.1 0.8 copy-done
  0.9 0.0 copy-start.3
  0.9 1.1 %copy-done.3 = bf16[8,152,152]{2,1,0:T(8,128)(2,1)S(1)} copy-done((bf16[8,152,152]{2,1,0:T(8,128)(2,1)S(1)}, bf16[8,152,152]{2,1,0:T(8,128)(2,1)}, u32[]{:S(2)}) %copy-start.3) | copy-done | bytes 369688
  2.0 0.0 copy-start.5
  2.0 1.0 %copy-done.5 = bf16[152,1024]{1,0:T(8,128)(2,1)S(1)} copy-done((bf16[152,1024]{1,0:T(8,128)(2,1)S(1)}, bf16[152,1024]{1,0:T(8,128)(2,1)}, u32[]{:S(2)}) %copy-start.5) | copy-done | bytes 311320
  3.0 0.0 copy-start.8
  3.0 1.0 %copy-done.8 = bf16[512,512]{1,0:T(8,128)(2,1)S(1)} copy-done((bf16[512,512]{1,0:T(8,128)(2,1)S(1)}, bf16[512,512]{1,0:T(8,128)(2,1)}, u32[]{:S(2)}) %copy-start.8) | copy-done | bytes 524312
  4.0 0.0 copy-start.1
  4.0 0.0 copy-start.10
  4.0 1.2 %prep.1 = (bf16[8,160,128]{2,1,0:T(8,128)(2,1)S(1)}, bf16[160,128]{1,0:T(8,128)(2,1)S(1)}, bf16[2,160,128]{2,1,0:T(8,128)(2,1)S(1)}, bf16[2,160,128]{2,1,0:T(8,128)(2,1)S(1)}) custom-call(s32[3]{0:T(128)S(1)} %pad_add_fusion.par, bf16[152,1024]{1,0:T(8,128)(2,1)S(1)} %copy-done.5, bf16[8,152,152]{2,1,0:T(8,128)(2,1)S(1)} %copy-done.3, ...), custom_call_target="tpu_custom_call" | custom-call | flops 1000000000 | bytes 2097152 | tf_op jit(solution)/shard_map/prep/pallas_call | solution.py:528
  5.3 0.1 collective-permute-start
  5.3 2.4 %collective-permute-start.1 = (bf16[2,160,128]{2,1,0:T(8,128)(2,1)S(1)}, bf16[2,160,128]{2,1,0:T(8,128)(2,1)S(1)}, u32[]{:S(2)}, u32[]{:S(2)}) collective-permute-start(bf16[2,160,128]{2,1,0:T(8,128)(2,1)S(1)} %get-tuple-element.23), channel_id=1, source_target_pairs={{1,8},{8,1},{3,10},{10,3},{5,12},{12,5},{7,14},{14,7},{17,24},{24,... | collective-permute-start | bytes 245768 | tf_op jit(solution)/shard_map/ppermute | solution.py:558
  7.8 0.0 collective-permute-done.got_a
  7.8 3.3 %collective-permute-done.1.got_b = bf16[2,160,128]{2,1,0:T(8,128)(2,1)S(1)} collective-permute-done((bf16[2,160,128]{2,1,0:T(8,128)(2,1)S(1)}, bf16[2,160,128]{2,1,0:T(8,128)(2,1)S(1)}, u32[]{:S(2)}, u32[]{:S(2)}) %collective-permute-start.1) | collective-permute-done | bytes 81952 | tf_op jit(solution)/shard_map/ppermute | solution.py:558
  11.1 1.0 %pack_y.1 = (bf16[8,160,128]{2,1,0:T(8,128)(2,1)S(1)}, bf16[160,128]{1,0:T(8,128)(2,1)S(1)}, bf16[5,160,128]{2,1,0:T(8,128)(2,1)S(1)}, bf16[5,160,128]{2,1,0:T(8,128)(2,1)S(1)}) custom-call(s32[3]{0:T(128)S(1)} %pad_add_fusion.par, bf16[8,160,128]{2,1,0:T(8,128)(2,1)S(1)} %get-tuple-element.20.own, bf16[160,128]{1,0:T(8,128)(2,1)S(1)} %get-tuple-element.21.coarse, ...), custom_call_target="tpu_custom_call" | custom-call | flops 1000000 | bytes 2097152 | tf_op jit(solution)/shard_map/pack_y/pallas_call | solution.py:528
  12.1 1.6 %collective-permute-start.2 = (bf16[5,160,128]{2,1,0:T(8,128)(2,1)S(1)}, bf16[5,160,128]{2,1,0:T(8,128)(2,1)S(1)}, u32[]{:S(2)}, u32[]{:S(2)}) collective-permute-start(bf16[5,160,128]{2,1,0:T(8,128)(2,1)S(1)} %get-tuple-element.26), channel_id=1, source_target_pairs={{0,2},{2,0},{1,3},{3,1},{4,6},{6,4},{5,7},{7,5},{8,10},{10,8},{9,1... | collective-permute-start | bytes 614408 | tf_op jit(solution)/shard_map/ppermute | solution.py:556
  13.6 2.2 %collective-permute-start.3 = (bf16[5,160,128]{2,1,0:T(8,128)(2,1)S(1)}, bf16[5,160,128]{2,1,0:T(8,128)(2,1)S(1)}, u32[]{:S(2)}, u32[]{:S(2)}) collective-permute-start(bf16[5,160,128]{2,1,0:T(8,128)(2,1)S(1)} %get-tuple-element.27), channel_id=1, source_target_pairs={{2,16},{16,2},{3,17},{17,3},{6,20},{20,6},{7,21},{21,7},{10,24},{2... | collective-permute-start | bytes 614408 | tf_op jit(solution)/shard_map/ppermute | solution.py:558
  15.8 2.7 %collective-permute-done.2.got_a = bf16[5,160,128]{2,1,0:T(8,128)(2,1)S(1)} collective-permute-done((bf16[5,160,128]{2,1,0:T(8,128)(2,1)S(1)}, bf16[5,160,128]{2,1,0:T(8,128)(2,1)S(1)}, u32[]{:S(2)}, u32[]{:S(2)}) %collective-permute-start.2) | collective-permute-done | bytes 204832 | tf_op jit(solution)/shard_map/ppermute | solution.py:556
  18.6 6.1 %collective-permute-done.3.got_b = bf16[5,160,128]{2,1,0:T(8,128)(2,1)S(1)} collective-permute-done((bf16[5,160,128]{2,1,0:T(8,128)(2,1)S(1)}, bf16[5,160,128]{2,1,0:T(8,128)(2,1)S(1)}, u32[]{:S(2)}, u32[]{:S(2)}) %collective-permute-start.3) | collective-permute-done | bytes 204832 | tf_op jit(solution)/shard_map/ppermute | solution.py:558
  24.7 0.0 copy-done.1
  24.7 1.9 %pack_x.1 = (bf16[8,160,128]{2,1,0:T(8,128)(2,1)S(1)}, bf16[8,160,128]{2,1,0:T(8,128)(2,1)S(1)}, bf16[160,128]{1,0:T(8,128)(2,1)S(1)}, bf16[160,128]{1,0:T(8,128...) custom-call(s32[3]{0:T(128)S(1)} %pad_add_fusion.par, ...), custom_call_target="tpu_custom_call" | custom-call | flops 1000000 | bytes 2097152 | tf_op jit(solution)/shard_map/pack_x/pallas_call | solution.py:528
  26.6 1.5 %collective-permute-start.4 = (bf16[9,160,128]{2,1,0:T(8,128)(2,1)S(1)}, bf16[9,160,128]{2,1,0:T(8,128)(2,1)S(1)}, u32[]{:S(2)}, u32[]{:S(2)}) collective-permute-start(bf16[9,160,128]{2,1,0:T(8,128)(2,1)S(1)} %get-tuple-element.32), channel_id=1, source_target_pairs={{0,4},{4,0},{1,5},{5,1},{2,6},{6,2},{3,7},{7,3},{8,12},{12,8},{9,1... | collective-permute-start | bytes 1105928 | tf_op jit(solution)/shard_map/ppermute | solution.py:556
  28.1 0.0 copy-done.10
  28.1 0.0 copy-start.2
  28.1 0.0 copy-start.9
  28.1 19.6 %operators.1 = (bf16[316,152,128]{2,1,0:T(8,128)(2,1)S(1)}, bf16[96,152,128]{2,1,0:T(8,128)(2,1)S(1)}) custom-call(bf16[152,152,316]{2,1,0:T(8,128)(2,1)} %bitcast.4, bf16[316,512]{1,0:T(8,128)(2,1)S(1)} %copy-done.10), custom_call_target="tpu_custom_call" | custom-call | flops 10000000000 | bytes 18874368 | tf_op jit(solution)/shard_map/operators/pallas_call | solution.py:586
  47.8 0.0 copy-start.13
  47.8 4.4 %copy-done.13 = bf16[316,152,128]{2,1,0:T(8,128)(2,1)} copy-done((bf16[316,152,128]{2,1,0:T(8,128)(2,1)}, bf16[316,152,128]{2,1,0:T(8,128)(2,1)S(1)}, u32[]{:S(2)}) %copy-start.13) | copy-done | bytes 12296216
  52.2 0.0 copy-done.2
  52.2 0.0 copy-done.9
  52.2 0.0 copy-start.4
  52.2 0.0 copy-start.6
  52.2 0.0 copy-start.7
  52.2 0.0 copy-start.11
  52.3 0.0 copy-start.12
  52.3 0.5 masks.1.keep
  52.8 0.0 collective-permute-done.4.got_a
  52.8 0.1 broadcast_in_dim.3.got_b
  52.8 0.5 copy-done.4
  53.3 0.0 copy-done.6
  53.3 0.0 copy-done.7
  53.3 0.0 copy-done.11
  53.4 0.0 copy-done.12
  53.4 37.7 %translate.1 = bf16[152,1024]{1,0:T(8,128)(2,1)} custom-call(s32[3]{0:T(128)S(1)} %pad_add_fusion.par, s32[2512]{0:T(1024)S(1)} %copy-done.11, s32[1456]{0:T(1024)S(1)} %copy-done.12, bf16[8,160,128]{2,1,0:T(8,128)(2,1)S(1)} %get-tuple-element.20.own, bf16[8,160,128]{2,1,0:T(8,128)(2,1)S(1)} %get-tuple-element.24.hz, ...), custom_call_target="tpu_custom_call" | custom-call | flops 20000000000 | bytes 20971520 | tf_op jit(solution)/shard_map/translate/pallas_call | solution.py:528
Async XLA Ops:
  0.1 0.8 copy-start
  0.9 1.1 %copy-start.3 = (bf16[8,152,152]{2,1,0:T(8,128)(2,1)S(1)}, bf16[8,152,152]{2,1,0:T(8,128)(2,1)}, u32[]{:S(2)}) copy-start(bf16[8,152,152]{2,1,0:T(8,128)(2,1)} %up.1) | copy-start | bytes 1108996
  2.0 1.0 %copy-start.5 = (bf16[152,1024]{1,0:T(8,128)(2,1)S(1)}, bf16[152,1024]{1,0:T(8,128)(2,1)}, u32[]{:S(2)}) copy-start(bf16[152,1024]{1,0:T(8,128)(2,1)} %mult.1) | copy-start | bytes 933892
  3.0 1.0 %copy-start.8 = (bf16[512,512]{1,0:T(8,128)(2,1)S(1)}, bf16[512,512]{1,0:T(8,128)(2,1)}, u32[]{:S(2)}) copy-start(bf16[512,512]{1,0:T(8,128)(2,1)} %constant.22.clone.hot) | copy-start | bytes 1572868
  4.0 20.7 %copy-start.1 = (f32[121,128]{1,0:T(8,128)S(1)}, f32[121,128]{1,0:T(8,128)}, u32[]{:S(2)}) copy-start(f32[121,128]{1,0:T(8,128)} %constant.23.clone.tab) | copy-start | bytes 185860
  4.0 24.1 %copy-start.10 = (bf16[316,512]{1,0:T(8,128)(2,1)S(1)}, bf16[316,512]{1,0:T(8,128)(2,1)}, u32[]{:S(2)}) copy-start(bf16[316,512]{1,0:T(8,128)(2,1)} %constant.24.clone.order) | copy-start | bytes 970756
  5.3 2.5 %collective-permute-start = (bf16[2,160,128]{2,1,0:T(8,128)(2,1)S(1)}, bf16[2,160,128]{2,1,0:T(8,128)(2,1)S(1)}, u32[]{:S(2)}, u32[]{:S(2)}) collective-permute-start(bf16[2,160,128]{2,1,0:T(8,128)(2,1)S(1)} %get-tuple-element.22), channel_id=1, source_target_pairs={{0,1},{1,0},{2,3},{3,2},{4,5},{5,4},{6,7},{7,6},{8,9},{9,8},{10,11... | collective-permute-start | bytes 245768 | tf_op jit(solution)/shard_map/ppermute | solution.py:556
  5.3 5.8 %collective-permute-start.1 = (bf16[2,160,128]{2,1,0:T(8,128)(2,1)S(1)}, bf16[2,160,128]{2,1,0:T(8,128)(2,1)S(1)}, u32[]{:S(2)}, u32[]{:S(2)}) collective-permute-start(bf16[2,160,128]{2,1,0:T(8,128)(2,1)S(1)} %get-tuple-element.23), channel_id=1, source_target_pairs={{1,8},{8,1},{3,10},{10,3},{5,12},{12,5},{7,14},{14,7},{17,24},{24,... | collective-permute-start | bytes 245768 | tf_op jit(solution)/shard_map/ppermute | solution.py:558
  12.1 6.5 %collective-permute-start.2 = (bf16[5,160,128]{2,1,0:T(8,128)(2,1)S(1)}, bf16[5,160,128]{2,1,0:T(8,128)(2,1)S(1)}, u32[]{:S(2)}, u32[]{:S(2)}) collective-permute-start(bf16[5,160,128]{2,1,0:T(8,128)(2,1)S(1)} %get-tuple-element.26), channel_id=1, source_target_pairs={{0,2},{2,0},{1,3},{3,1},{4,6},{6,4},{5,7},{7,5},{8,10},{10,8},{9,1... | collective-permute-start | bytes 614408 | tf_op jit(solution)/shard_map/ppermute | solution.py:556
  13.6 11.0 %collective-permute-start.3 = (bf16[5,160,128]{2,1,0:T(8,128)(2,1)S(1)}, bf16[5,160,128]{2,1,0:T(8,128)(2,1)S(1)}, u32[]{:S(2)}, u32[]{:S(2)}) collective-permute-start(bf16[5,160,128]{2,1,0:T(8,128)(2,1)S(1)} %get-tuple-element.27), channel_id=1, source_target_pairs={{2,16},{16,2},{3,17},{17,3},{6,20},{20,6},{7,21},{21,7},{10,24},{2... | collective-permute-start | bytes 614408 | tf_op jit(solution)/shard_map/ppermute | solution.py:558
  26.6 26.2 %collective-permute-start.4 = (bf16[9,160,128]{2,1,0:T(8,128)(2,1)S(1)}, bf16[9,160,128]{2,1,0:T(8,128)(2,1)S(1)}, u32[]{:S(2)}, u32[]{:S(2)}) collective-permute-start(bf16[9,160,128]{2,1,0:T(8,128)(2,1)S(1)} %get-tuple-element.32), channel_id=1, source_target_pairs={{0,4},{4,0},{1,5},{5,1},{2,6},{6,2},{3,7},{7,3},{8,12},{12,8},{9,1... | collective-permute-start | bytes 1105928 | tf_op jit(solution)/shard_map/ppermute | solution.py:556
  28.1 24.1 %copy-start.2 = (s32[316,1024]{1,0:T(8,128)S(1)}, s32[316,1024]{1,0:T(8,128)}, u32[]{:S(2)}) copy-start(s32[316,1024]{1,0:T(8,128)} %fine.1) | copy-start | bytes 3883012
  28.1 24.1 %copy-start.9 = (bf16[512,512]{1,0:T(8,128)(2,1)S(1)}, bf16[512,512]{1,0:T(8,128)(2,1)}, u32[]{:S(2)}) copy-start(bf16[512,512]{1,0:T(8,128)(2,1)} %constant.22.clone.hot) | copy-start | bytes 1572868
  47.8 4.5 %copy-start.13 = (bf16[316,152,128]{2,1,0:T(8,128)(2,1)}, bf16[316,152,128]{2,1,0:T(8,128)(2,1)S(1)}, u32[]{:S(2)}) copy-start(bf16[316,152,128]{2,1,0:T(8,128)(2,1)S(1)} %get-tuple-element.33.main) | copy-start | bytes 36888580
  52.2 1.1 %copy-start.4 = (bf16[8,152,152]{2,1,0:T(8,128)(2,1)S(1)}, bf16[8,152,152]{2,1,0:T(8,128)(2,1)}, u32[]{:S(2)}) copy-start(bf16[8,152,152]{2,1,0:T(8,128)(2,1)} %down.1) | copy-start | bytes 1108996
  52.2 1.1 %copy-start.6 = (s32[316,128]{1,0:T(8,128)S(1)}, s32[316,128]{1,0:T(8,128)}, u32[]{:S(2)}) copy-start(s32[316,128]{1,0:T(8,128)} %clist.1) | copy-start | bytes 485380
  52.2 1.1 %copy-start.7 = (bf16[152,152]{1,0:T(8,128)(2,1)S(1)}, bf16[152,152]{1,0:T(8,128)(2,1)}, u32[]{:S(2)}) copy-start(bf16[152,152]{1,0:T(8,128)(2,1)} %inverse.1) | copy-start | bytes 138628
  52.2 1.1 %copy-start.11 = (s32[2512]{0:T(1024)S(1)}, s32[2512]{0:T(1024)}, u32[]{:S(2)}) copy-start(s32[2512]{0:T(1024)} %constant.25.clone.ft) | copy-start | bytes 30148
  52.3 1.1 %copy-start.12 = (s32[1456]{0:T(1024)S(1)}, s32[1456]{0:T(1024)}, u32[]{:S(2)}) copy-start(s32[1456]{0:T(1024)} %constant.26.clone.ct) | copy-start | bytes 17476

commit v2 on v1

--- a/solution.py
+++ b/solution.py
@@ -1,3 +1,4 @@
+import functools
 import itertools
 
 import jax
@@ -103,6 +104,15 @@
                         if not 0 <= moved[axis] < EXT[axis]:
                             lanes.add(lane_of(moved))
                     masks.add(("stage", depth, axis, kind, step), lanes)
+    for d in itertools.product((-1, 0, 1), repeat=3):
+        for axis in range(3):
+            lanes = set()
+            for e in itertools.product(*map(range, EXT)):
+                moved = [e[n] + d[n] for n in range(3)]
+                if not 0 <= moved[axis] < EXT[axis]:
+                    lanes.add(lane_of(moved))
+            if d[axis]:
+                masks.add(("out", d, axis), lanes)
     for s in range(8):
         masks.add(("zpack", s), {l for l in every if l % PZ == s})
     row = PY * PZ
@@ -116,6 +126,13 @@
     masks.add(("xsrc_a", 1), set(range(LANES - row, LANES)))
     for side, i in ((0, 0), (1, PX - 1)):
         masks.add(("xsrc_b", side), {lane_of((i, j, k)) for j in range(PY) for k in (-1, PZ)})
+    for side, i in ((0, (0, 1)), (1, (PX - 2, PX - 1))):
+        masks.add(
+            ("cy", side),
+            {lane_of((n, j, k)) for n in i for j in (-2, -1, PY, PY + 1) for k in range(PZ)},
+        )
+    masks.add("half", {l for l in every if l < LANES // 2})
+    masks.add("mid", {l for l in every if 2 <= l % PZ < 6})
     for t in range(2):
         masks.add(("xpack_a", t), {l for l in every if l // 64 == t})
     for t in range(8):
@@ -132,6 +149,15 @@
     n = MASKS.rows[name]
     row = jnp.broadcast_to(tab[n : n + 1, :], yes.shape).astype(BF)
     return jnp.where(row > 0, yes, no)
+
+
+def pick_row(tab, n, yes, no):
+    row = jnp.broadcast_to(tab[pl.ds(n, 1), :], yes.shape).astype(BF)
+    return jnp.where(row > 0, yes, no)
+
+
+def turn_by(x, by):
+    return pltpu.roll(x, lax.rem(by + 4 * LANES, LANES), 1)
 
 
 def roll(x, by):
@@ -163,10 +189,24 @@
     return halves
 
 
-def prep_kernel(par, mult, up, hot, tab, own, coarse, send_a, send_b):
+def prep_kernel(
+    par, mult_hbm, up_hbm, hot_hbm, tab_hbm, own, coarse, send_a, send_b, mult, up, hot, tab, sems
+):
+    copies = [
+        pltpu.make_async_copy(src, dst, sems.at[n])
+        for n, (src, dst) in enumerate(
+            ((mult_hbm, mult), (hot_hbm, hot), (up_hbm, up), (tab_hbm, tab))
+        )
+    ]
+    for copy in copies:
+        copy.start()
     chans = mult.shape[0]
     rows = own.shape[1]
+    copies[0].wait()
+    copies[1].wait()
     halves = to_octants(mult[...], hot[...])
+    copies[2].wait()
+    copies[3].wait()
     total = jnp.zeros((chans, LANES), F32)
     pack = [None, None]
     for s in range(8):
@@ -220,7 +260,7 @@
         send[4] = far
 
 
-def x_kernel(par, own, coarse, hz, cz, got_a, got_b, tab, hy, hyz, cy, cyz, send_a, send_b):
+def x_kernel(par, own, coarse, hz, cz, got_a, got_b, tab, hy, hyz, cy, cyz, *sends):
     row = PY * PZ
     for s in range(8):
         block, t = s // 3, s % 3
@@ -235,29 +275,61 @@
         near.append(pick(tab, ("plus", 2, kind, 1), roll(p, row), roll(m, -row)))
     cy[...] = near[0]
     cyz[...] = near[1]
-    even = par[0] == 0
-    pack_a = [[None] * 4, [None] * 4]
-    pack_b = [None, None]
-    for s in range(8):
-        block, t = s // 2, s % 2
-        u, v = s % 4, s // 4
-        for side in range(2):
-            a = pick(tab, ("xsrc_a", side), own[s], hy[s])
-            b = pick(tab, ("xsrc_b", side), hz[s], hyz[s])
-            a = roll(a, 8 + 64 * t - (PX - 1) * row * side)
-            b = roll(b, 9 + 2 * u + 64 * v - (PX - 1) * row * side)
-            pack_a[side][block] = a if t == 0 else pick(tab, ("xpack_a", t), a, pack_a[side][block])
-            pack_b[side] = b if s == 0 else pick(tab, ("xpack_b", s), b, pack_b[side])
-    for block in range(4):
-        send_a[block] = jnp.where(even, pack_a[1][block], pack_a[0][block])
-        send_b[block] = jnp.where(even, pack_a[0][block], pack_a[1][block])
-    send_a[4] = jnp.where(even, pack_b[1], pack_b[0])
-    send_b[4] = jnp.where(even, pack_b[0], pack_b[1])
-    for send in (send_a, send_b):
-        send[5] = coarse[...]
-        send[6] = near[0]
-        send[7] = cz[...]
-        send[8] = near[1]
+    half = LANES // 2
+    other = roll(near[0], half)
+    low = pick(tab, "half", coarse[...], pick(tab, ("cy", 0), near[0], other))
+    high = pick(tab, "half", pick(tab, ("cy", 1), near[0], other), coarse[...])
+    edges = pick(tab, "mid", roll(near[1], 4), cz[...])
+    for send, odd in zip(sends, (0, 1)):
+        side = par[0] if odd else 1 - par[0]
+        far = (PX - 1) * row * side
+        whole, line = [None] * 4, None
+        for s in range(8):
+            block, t = s // 2, s % 2
+            u, v = s % 4, s // 4
+            a = pick_row(tab, MASKS.rows["xsrc_a", 0] + side, own[s], hy[s])
+            b = pick_row(tab, MASKS.rows["xsrc_b", 0] + side, hz[s], hyz[s])
+            a = turn_by(a, 8 + 64 * t - far)
+            b = turn_by(b, 9 + 2 * u + 64 * v - far)
+            whole[block] = a if t == 0 else pick(tab, ("xpack_a", t), a, whole[block])
+            line = b if s == 0 else pick(tab, ("xpack_b", s), b, line)
+        for block in range(4):
+            send[block] = whole[block]
+        send[4] = line
+        send[5] = jnp.where(side == 1, high, low)
+        send[6] = edges
+
+
+def planes(tab, kinds, far, plane):
+    for dy in range(-3, 4):
+        y = {
+            z: shifted(tab, 2, 1, (0, 0, z), dy, kinds[far, 0, z], kinds[far, 1, z])
+            for z in (0, 1)
+        }
+        for dz in range(-3, 4):
+            plane[(dy + 3) * 7 + dz + 3, :, far * LANES : (far + 1) * LANES] = shifted(
+                tab, 2, 2, (0, 0, 0), dz, y[0], y[1]
+            )
+
+
+def put_slots(tab, s, kinds, slots, steps):
+    for d in steps:
+        n = ((d[0] + 1) * 9 + (d[1] + 1) * 3 + d[2] + 1) * 8 + s
+        by = d[0] * PY * PZ + d[1] * PZ + d[2]
+        slots[n] = roll(gathered(tab, d, kinds, ()), -by)
+
+
+def early_kernel(own, hz, hy, hyz, coarse, cz, cy, cyz, tab, slots, plane):
+    kinds = {(0, 0, 0): coarse[...], (0, 1, 0): cy[...], (0, 0, 1): cz[...], (0, 1, 1): cyz[...]}
+    planes(tab, kinds, 0, plane)
+    steps = [(0, dy, dz) for dy in (-1, 0, 1) for dz in (-1, 0, 1) if dy or dz]
+
+    def body(s, carry):
+        kinds = {(0, 0, 0): own[s], (0, 1, 0): hy[s], (0, 0, 1): hz[s], (0, 1, 1): hyz[s]}
+        put_slots(tab, s, kinds, slots, steps)
+        return carry
+
+    lax.fori_loop(0, 8, body, 0)
 
 
 def offset_sets():
@@ -265,8 +337,10 @@
 
     def add(offsets):
         start = len(fours)
-        for n in range(0, len(offsets), 4):
-            fours.append(tuple(offsets[n : n + 4]))
+        for turn in range(PX):
+            like = [d for d in offsets if d[0] % PX == turn]
+            for n in range(0, len(like), 4):
+                fours.append(tuple(like[n : n + 4]))
         return list(range(start, len(fours)))
 
     small = range(-2, 3)
@@ -338,15 +412,37 @@
 
 
 def coarse_table(spare):
+    chunks = []
+    for turn in range(PX):
+        offsets = [d for d in SHIFTS if d[0] % PX == turn]
+        fours = [n for n, four in enumerate(FOURS) if four[0][0] % PX == turn]
+        parts = 1 if turn == 0 else 2
+        cut, cut4 = -(-len(offsets) // parts), -(-len(fours) // parts)
+        for part in range(parts):
+            chunks.append(
+                (turn, offsets[part * cut : (part + 1) * cut], fours[part * cut4 : (part + 1) * cut4])
+            )
+    count = max(len(c[1]) for c in chunks)
+    count4 = max(len(c[2]) for c in chunks)
+    count += (count + count4) % 2
+
+    def entry(d):
+        if d is None:
+            return [0, spare, 24]
+        return [NUMBER[d], NUMBER[d], (d[1] + 3) * 7 + d[2] + 3]
+
     rows = []
-    for four in FOURS:
-        for n in range(4):
-            d = four[n] if n < len(four) else None
-            if d is None:
-                rows.append((0, spare, 3 * 7 + 3, 0))
-            else:
-                rows.append((NUMBER[d], NUMBER[d], (d[0] + 3) * 7 + d[1] + 3, d[2] + 3))
-    return np.array(rows, np.int32)
+    for turn, offsets, fours in chunks:
+        row = [turn]
+        for n in range(count):
+            row += entry(offsets[n] if n < len(offsets) else None)
+        for n in range(count4):
+            four = FOURS[fours[n]] if n < len(fours) else ()
+            row.append(fours[n] if n < len(fours) else 0)
+            for place in range(4):
+                row += entry(four[place] if place < len(four) else None)
+        rows.append(row)
+    return np.array(rows, np.int32), count, count4
 
 
 def rest_order(offsets):
@@ -357,20 +453,51 @@
     return hot
 
 
-def operator_kernel(w, order, main, rest):
-    block, chans, offsets = w.shape
-    at = pl.multiple_of(pl.program_id(0) * block, block)
-    main[:, pl.ds(at, block), :] = jnp.transpose(w[:, 0:LANES, :], (2, 0, 1))
+DEPTH = 6
+
+
+def main_operator_kernel(first, blocks, w, *refs):
+    main, held, sems = refs[-3:]
+
+    def copy(n):
+        at = pl.multiple_of((first + n) * 8, 8)
+        slot = lax.rem(n, DEPTH)
+        return pltpu.make_async_copy(w.at[pl.ds(at, 8), 0:LANES, :], held.at[slot], sems.at[slot])
+
+    for n in range(DEPTH - 1):
+        copy(n).start()
+
+    def body(n, carry):
+        @pl.when(n + DEPTH - 1 < blocks)
+        def _():
+            copy(n + DEPTH - 1).start()
+
+        copy(n).wait()
+        at = pl.multiple_of((first + n) * 8, 8)
+        main[:, pl.ds(at, 8), :] = jnp.transpose(held[lax.rem(n, DEPTH)], (2, 0, 1))
+        return carry
+
+    lax.fori_loop(0, blocks, body, 0)
+
+
+def rest_operator_kernel(w, order, rest, held, sem):
+    chans, _, offsets = w.shape
     left = chans - LANES
-    stacked = []
-    for n in range(block):
-        y = jnp.dot(w[n, LANES:chans, :], order[...], preferred_element_type=F32).astype(BF)
-        y = padded(y, 32)
-        stacked.append(
-            jnp.concatenate([y[:, m * LANES : (m + 1) * LANES] for m in range(4)], 0)
-        )
-    turned = jnp.transpose(jnp.stack(stacked), (2, 0, 1))
-    rest[:, pl.ds(at, block), :] = turned[0 : rest.shape[0]]
+    whole = pltpu.make_async_copy(w.at[:, LANES:chans, :], held, sem)
+    whole.start()
+    whole.wait()
+
+    for at in range(0, chans, 8):
+        y = held[pl.ds(at, 8)].reshape(8 * left, offsets)
+        y = jnp.dot(y, order[...], preferred_element_type=F32).astype(BF)
+        stacked = []
+        for m in range(8):
+            part = padded(y[m * left : (m + 1) * left], 32)
+            stacked.append(
+                jnp.concatenate([part[:, f * LANES : (f + 1) * LANES] for f in range(4)], 0)
+            )
+        turned = jnp.transpose(jnp.stack(stacked), (2, 0, 1))
+        rest[:, pl.ds(at, 8), :] = turned[0 : rest.shape[0]]
 
 
 def mask_kernel(fine, hot, out):
@@ -388,6 +515,16 @@
     return roll(pick(tab, ("stage", depth, axis, kind, step), outside, inside), -step * stride)
 
 
+def gathered(tab, d, kinds, done):
+    axis = len(done)
+    if axis == 3:
+        return kinds[done]
+    inside = gathered(tab, d, kinds, done + (0,))
+    if d[axis] == 0:
+        return inside
+    return pick(tab, ("out", d, axis), gathered(tab, d, kinds, done + (1,)), inside)
+
+
 def dot_pieces(pieces):
     left = jnp.concatenate([p[0] for p in pieces], 1)
     right = jnp.concatenate([p[1] for p in pieces], 0)
@@ -395,73 +532,95 @@
 
 
 def main_kernel(
-    par, ft, ct, own, hz, hy, hyz, coarse, cz, cy, cyz, got_a, got_b, tab, main, rest, keep, clist,
-    down, inverse, hot, out, slots, acc, cacc, plane, cmask,
+    form, par, ft, ct, own, hz, hy, hyz, got_a, got_b, tab, outside, main, rest, keep, clist,
+    down, inverse, hot, _slots, _plane, out, slots, plane, acc, cacc, cmask,
 ):
     chans = acc.shape[1]
     rows = own.shape[1]
     row = PY * PZ
-    for s in range(8):
+    kinds = {}
+    p, m = sides(par, 0, got_a[5], got_b[5])
+    py, my = roll(p, LANES // 2), roll(m, LANES // 2)
+    pz, mz = sides(par, 0, got_a[6], got_b[6])
+    arrived = {
+        (0, 0, 0): (p, m),
+        (0, 1, 0): (pick(tab, "half", py, p), pick(tab, "half", m, my)),
+        (0, 0, 1): (pz, mz),
+        (0, 1, 1): (roll(pz, -4), roll(mz, -4)),
+    }
+    for k in KINDS_YZ:
+        far = (1, k[1], k[2])
+        kinds[far] = pick(tab, ("plus", 2, far, 0), *arrived[k])
+    planes(tab, kinds, 1, plane)
+    offsets = clist.shape[0]
+    present = padded((clist[...] >= 0).astype(F32), cmask.shape[1])
+    for turn in range(PX):
+        turned = roll(present, turn * row)
+        cmask[turn, :, 0:LANES] = turned * (1 - outside[...])
+        cmask[turn, :, LANES:] = turned * outside[...]
+    acc[...] = jnp.zeros_like(acc)
+    cacc[...] = jnp.zeros_like(cacc)
+
+    def fine_sources(s):
         block, t = s // 2, s % 2
         u, v = s % 4, s // 4
-        p, m = sides(par, 0, got_a[block], got_b[block])
-        p, m = roll(p, -8 - 64 * t), roll(m, -8 - 64 * t + (PX - 1) * row)
-        hx = pick(tab, ("plus", 1, (1, 0, 0), 0), p, m)
-        hxy = pick(tab, ("plus", 1, (1, 1, 0), 0), p, m)
-        p, m = sides(par, 0, got_a[4], got_b[4])
-        p, m = roll(p, -9 - 2 * u - 64 * v), roll(m, -9 - 2 * u - 64 * v + (PX - 1) * row)
-        hxz = pick(tab, ("plus", 1, (1, 0, 1), 0), p, m)
-        hxyz = pick(tab, ("plus", 1, (1, 1, 1), 0), p, m)
-        inner = {(0, 0, 0): own[s], (0, 1, 0): hy[s], (0, 0, 1): hz[s], (0, 1, 1): hyz[s]}
-        outer = {(0, 0, 0): hx, (0, 1, 0): hxy, (0, 0, 1): hxz, (0, 1, 1): hxyz}
-        for dx in (-1, 0, 1):
-            x = {k: shifted(tab, 1, 0, k, dx, inner[k], outer[k]) for k in KINDS_YZ}
-            for dy in (-1, 0, 1):
-                y = {
-                    z: shifted(tab, 1, 1, (0, 0, z), dy, x[0, 0, z], x[0, 1, z]) for z in (0, 1)
-                }
-                for dz in (-1, 0, 1):
-                    n = ((dx + 1) * 9 + (dy + 1) * 3 + dz + 1) * 8 + s
-                    slots[n] = shifted(tab, 1, 2, (0, 0, 0), dz, y[0], y[1])
-    inner = {(0, 0, 0): coarse[...], (0, 1, 0): cy[...], (0, 0, 1): cz[...], (0, 1, 1): cyz[...]}
-    outer = {}
-    for n, k in ((5, (0, 0, 0)), (6, (0, 1, 0)), (7, (0, 0, 1)), (8, (0, 1, 1))):
-        p, m = sides(par, 0, got_a[n], got_b[n])
-        outer[k] = pick(tab, ("plus", 2, (1, k[1], k[2]), 0), p, m)
-    for dx in range(-3, 4):
-        x = {k: shifted(tab, 2, 0, k, dx, inner[k], outer[k]) for k in KINDS_YZ}
-        for dy in range(-3, 4):
-            for z in (0, 1):
-                plane[((dx + 3) * 7 + dy + 3) * 2 + z] = shifted(
-                    tab, 2, 1, (0, 0, z), dy, x[0, 0, z], x[0, 1, z]
-                )
-    offsets = clist.shape[0]
-    cmask[...] = jnp.zeros_like(cmask)
-    cmask[0:offsets, :] = (clist[...] >= 0).astype(F32)
-    acc[...] = jnp.zeros_like(acc)
-    cacc[...] = jnp.zeros_like(cacc)
-    first = MASKS.rows["stage", 2, 2, (0, 0, 0), -3]
-
-    def coarse_body(it, carry):
+        far = (PX - 1) * row
+
+        at_a, at_b = -8 - 64 * t, -9 - 2 * u - 64 * v
+        if form[3]:
+            hx = hxy = turn_by(got_a[block], at_a + far * par[0])
+            hxz = hxyz = turn_by(got_a[4], at_b + far * par[0])
+        else:
+            p, m = sides(par, 0, got_a[block], got_b[block])
+            p, m = turn_by(p, at_a), turn_by(m, at_a + far)
+            hx = pick(tab, ("plus", 1, (1, 0, 0), 0), p, m)
+            hxy = pick(tab, ("plus", 1, (1, 1, 0), 0), p, m)
+            p, m = sides(par, 0, got_a[4], got_b[4])
+            p, m = turn_by(p, at_b), turn_by(m, at_b + far)
+            hxz = pick(tab, ("plus", 1, (1, 0, 1), 0), p, m)
+            hxyz = pick(tab, ("plus", 1, (1, 1, 1), 0), p, m)
+        kinds = {
+            (0, 0, 0): own[s], (0, 1, 0): hy[s], (0, 0, 1): hz[s], (0, 1, 1): hyz[s],
+            (1, 0, 0): hx, (1, 1, 0): hxy, (1, 0, 1): hxz, (1, 1, 1): hxyz,
+        }
+        steps = [d for d in itertools.product((-1, 0, 1), repeat=3) if d[0]]
+        put_slots(tab, s, kinds, slots, steps)
+
+    def coarse_chunk(c):
+        base = c * form[2]
+        turn = ct[base]
+
+        def source(at, lo, hi):
+            md, pn = ct[at + 1], ct[at + 2]
+            shape = (hi - lo, 2 * LANES)
+            mask = jnp.broadcast_to(cmask[turn, pl.ds(md, 1), :], shape).astype(BF)
+            return plane[pn, lo:hi] * mask
+
+        at = base + 1
         pieces = []
-        for f in range(7):
+        for n in range(form[0]):
+            pieces.append((main[ct[at]], source(at, 0, LANES)))
+            at = at + 3
+        for n in range(form[1]):
+            four = ct[at]
+            at = at + 1
             rests = []
-            four = it * 7 + f
-            for n in range(4):
-                at = (four * 4 + n) * 4
-                d, md, pn, dz = ct[at], ct[at + 1], ct[at + 2], ct[at + 3]
-                far = jnp.broadcast_to(tab[pl.ds(first + dz, 1), :], (rows, LANES)).astype(BF)
-                src = jnp.where(far > 0, plane[pn * 2 + 1], plane[pn * 2])
-                src = pltpu.roll(src, LANES + 3 - dz, 1)
-                mask = jnp.broadcast_to(cmask[pl.ds(md, 1), :], (rows, LANES)).astype(BF)
-                x = src * mask
-                pieces.append((main[d], x[0:LANES]))
-                rests.append(x[LANES:rows])
+            for place in range(4):
+                rests.append(source(at, LANES, rows))
+                at = at + 3
             pieces.append((rest[four], jnp.concatenate(rests, 0)))
-        cacc[...] += dot_pieces(pieces)
+        cacc[turn] += dot_pieces(pieces)
+
+    chunks = ct.shape[0] // form[2]
+    for s in range(chunks, 8):
+        fine_sources(s)
+
+    def both(n, carry):
+        fine_sources(n)
+        coarse_chunk(n)
         return carry
 
-    lax.fori_loop(0, len(FOURS) // 7, coarse_body, 0)
+    lax.fori_loop(0, chunks, both, 0)
 
     def fine_body(j, carry):
         at = j * FINE_TABLE.shape[1]
@@ -500,7 +659,10 @@
         return carry
 
     lax.fori_loop(0, 4, fine_body, 0)
-    local = (0.5 * cacc[...]).astype(BF)
+    check = jnp.zeros(cacc.shape[1:2] + (LANES,), F32)
+    for turn in range(PX):
+        check = check + roll(cacc[turn, :, 0:LANES] + cacc[turn, :, LANES:], -turn * row)
+    local = (0.5 * check).astype(BF)
     total = []
     for s in range(8):
         spread = jnp.dot(down[s], local, preferred_element_type=F32)
@@ -521,20 +683,25 @@
 
 VMEM = pl.BlockSpec(memory_space=pltpu.VMEM)
 SMEM = pl.BlockSpec(memory_space=pltpu.SMEM)
-
-
-def call(kernel, name, smem, operands, outs, limit, scratch=(), flops=0, bytes_=0):
+HBM = pl.BlockSpec(memory_space=pltpu.MemorySpace.HBM)
+
+
+def call(kernel, name, smem, operands, outs, limit, scratch=(), flops=0, bytes_=0, hbm=(), aliases={}):
     shapes = [jax.ShapeDtypeStruct(s, t) for s, t in outs]
     return pl.pallas_call(
         kernel,
         name=name,
-        in_specs=[SMEM] * smem + [VMEM] * (len(operands) - smem),
+        in_specs=[SMEM if n < smem else HBM if n in hbm else VMEM for n in range(len(operands))],
         out_specs=[VMEM] * len(shapes),
         out_shape=shapes,
         scratch_shapes=list(scratch),
+        input_output_aliases=aliases,
         compiler_params=pltpu.CompilerParams(vmem_limit_bytes=limit),
         cost_estimate=pl.CostEstimate(flops=flops, bytes_accessed=bytes_, transcendentals=0),
-    )(*operands)
+    )(*[
+        pltpu.with_memory_space_constraint(x, pltpu.MemorySpace.HBM) if n in hbm else x
+        for n, x in enumerate(operands)
+    ])
 
 
 def local(
@@ -555,7 +722,7 @@
     def exchange(axis, a, b):
         got_a = lax.ppermute(a, "curve", swap_pairs(devices, levels, axis, 0))
         pairs = swap_pairs(devices, levels, axis, 1)
-        got_b = lax.ppermute(b, "curve", pairs) if pairs else jnp.zeros_like(b)
+        got_b = lax.ppermute(b, "curve", pairs) if pairs else got_a
         return got_a, got_b
 
     full = ((8, rows, LANES), BF)
@@ -563,60 +730,81 @@
     own, coarse, a, b = call(
         prep_kernel, "prep", 1, (par, multipole, upward_maps, hot, tab),
         [full, one, ((2, rows, LANES), BF), ((2, rows, LANES), BF)], 16 * MIB,
-        flops=10**9, bytes_=2 * MIB,
+        flops=10**9, bytes_=2 * MIB, hbm=(1, 2, 3, 4),
+        scratch=[
+            pltpu.VMEM(multipole.shape, BF),
+            pltpu.VMEM(upward_maps.shape, BF),
+            pltpu.VMEM(hot.shape, BF),
+            pltpu.VMEM(tab.shape, F32),
+            pltpu.SemaphoreType.DMA((4,)),
+        ],
     )
     za, zb = exchange(2, a, b)
+    rests = (len(FOURS) + 7) // 8 * 8
+    turned = jnp.transpose(transfer_maps, (1, 2, 0))
+    order = jnp.asarray(rest_order(offsets), BF)
+    blocks = chans // 8
+
+    def turn(first, count, *given):
+        (main,) = call(
+            functools.partial(main_operator_kernel, first, count), "main_operators", 0,
+            (turned, *given), [((offsets, chans, LANES), BF)], 10 * MIB,
+            flops=count * 25 * 10**7, bytes_=count * MIB, hbm=(0,), aliases={1: 0} if given else {},
+            scratch=[
+                pltpu.VMEM((DEPTH, 8, LANES, offsets), BF), pltpu.SemaphoreType.DMA((DEPTH,)),
+            ],
+        )
+        return main
+
+    ready = 2 * blocks // 5
+    main = turn(0, ready)
+    za, zb, main = lax.optimization_barrier((za, zb, main))
     hz, cz, a, b = call(
         y_kernel, "pack_y", 1, (par, own, coarse, za, zb, tab),
         [full, one, ((5, rows, LANES), BF), ((5, rows, LANES), BF)], 16 * MIB,
         flops=10**6, bytes_=2 * MIB,
     )
     ya, yb = exchange(1, a, b)
-    hy, hyz, cy, cyz, a, b = call(
+    main = turn(ready, blocks - ready, main)
+    ya, yb, main = lax.optimization_barrier((ya, yb, main))
+    lone = not swap_pairs(devices, levels, 0, 1)
+    hy, hyz, cy, cyz, *sends = call(
         x_kernel, "pack_x", 1, (par, own, coarse, hz, cz, ya, yb, tab),
-        [full, full, one, one, ((9, rows, LANES), BF), ((9, rows, LANES), BF)], 16 * MIB,
+        [full, full, one, one] + [((7, rows, LANES), BF)] * (1 if lone else 2), 16 * MIB,
         flops=10**6, bytes_=2 * MIB,
     )
-    xa, xb = exchange(0, a, b)
-
-    block = 8
-    rests = (len(FOURS) + 7) // 8 * 8
-    turned = jnp.transpose(transfer_maps, (1, 2, 0))
-    order = jnp.asarray(rest_order(offsets), BF)
-    main, rest = pl.pallas_call(
-        operator_kernel,
-        name="operators",
-        grid=(chans // block,),
-        in_specs=[
-            pl.BlockSpec((block, chans, offsets), lambda n: (n, 0, 0)),
-            pl.BlockSpec(order.shape, lambda n: (0, 0)),
-        ],
-        out_specs=[VMEM, VMEM],
-        out_shape=[
-            jax.ShapeDtypeStruct((offsets, chans, LANES), BF),
-            jax.ShapeDtypeStruct((rests, chans, LANES), BF),
-        ],
-        compiler_params=pltpu.CompilerParams(vmem_limit_bytes=30 * MIB),
-        cost_estimate=pl.CostEstimate(flops=10**10, bytes_accessed=18 * MIB, transcendentals=0),
-    )(turned, order)
+    xa, xb = exchange(0, sends[0], sends[-1])
+    (rest,) = call(
+        rest_operator_kernel, "rest_operators", 0, (turned, order), [((rests, chans, LANES), BF)],
+        8 * MIB, flops=5 * 10**9, bytes_=5 * MIB, hbm=(0,),
+        scratch=[pltpu.VMEM((chans, chans - LANES, offsets), BF), pltpu.SemaphoreType.DMA],
+    )
+
+    early = [((216, rows, LANES), BF), ((49, rows, 2 * LANES), BF)]
+    slots, plane = call(
+        early_kernel, "early", 0, (own, hz, hy, hyz, coarse, cz, cy, cyz, tab), early, 8 * MIB,
+        flops=10**9, bytes_=8 * MIB,
+    )
     (keep,) = call(
         mask_kernel, "masks", 0, (fine_lists, hot), [((8, row_pad, LANES), F32)], 16 * MIB,
         flops=10**9, bytes_=2 * MIB,
     )
+    xa, xb, slots, plane, keep, rest = lax.optimization_barrier((xa, xb, slots, plane, keep, rest))
     ft = jnp.asarray(FINE_TABLE.reshape(-1))
-    ct = jnp.asarray(coarse_table(row_pad - 1).reshape(-1))
-    (out,) = call(
-        main_kernel, "translate", 3,
-        (par, ft, ct, own, hz, hy, hyz, coarse, cz, cy, cyz, xa, xb, tab, main, rest, keep,
-         coarse_lists, downward_maps, check_inverse, hot),
-        [((chans, multipole.shape[1]), BF)],
-        44 * MIB,
+    table, count, count4 = coarse_table(row_pad - 1)
+    beyond = [TABLE[MASKS.rows["stage", 2, 0, (0, 0, 0), d[0]]] for d in SHIFTS]
+    outside = jnp.asarray(np.stack(beyond + [0 * beyond[0]] * (row_pad - offsets)))
+    ct = jnp.asarray(table.reshape(-1))
+    out, _, _ = call(
+        functools.partial(main_kernel, (count, count4, table.shape[1], lone)), "translate", 3,
+        (par, ft, ct, own, hz, hy, hyz, xa, xb, tab, outside, main, rest, keep,
+         coarse_lists, downward_maps, check_inverse, hot, slots, plane),
+        [((chans, multipole.shape[1]), BF), *early],
+        14 * MIB, aliases={18: 1, 19: 2},
         scratch=[
-            pltpu.VMEM((216, rows, LANES), BF),
             pltpu.VMEM((8, chans, LANES), F32),
-            pltpu.VMEM((chans, LANES), F32),
-            pltpu.VMEM((98, rows, LANES), BF),
-            pltpu.VMEM((row_pad, LANES), F32),
+            pltpu.VMEM((PX, chans, 2 * LANES), F32),
+            pltpu.VMEM((PX, row_pad, 2 * LANES), F32),
         ],
         flops=2 * 10**10, bytes_=20 * MIB,
     )

time: 91.7 us -> 61.3 us (0.67)
  Pallas kernels: 61.9 us -> 47.3 us
  local copies, waits for them, and re-layouts: 8.96 us -> 0.06 us
  waiting for transfers between devices: 12.1 us -> 5.64 us
    pallas_call x6 -> x9, Pallas kernels: 61.9 us -> 47.3 us  [call(): pl.pallas_call(kernel, name=name, in_specs=[SMEM if n < smem else HBM if...]
    unnamed x28 -> x20, local copies, waits for them, and re-layouts: 8.91 us -> 0.06 us
    ppermute x2, waiting for transfers between devices: 9.41 us -> 5.63 us  [exchange(): got_b = lax.ppermute(b, 'curve', pairs) if pairs else got_a]
    ppermute x3, waiting for transfers between devices: 2.73 us -> 0.01 us  [exchange(): got_a = lax.ppermute(a, 'curve', swap_pairs(devices, levels, axis, 0))]
  transfers between devices with their start and end apart: 5 -> 5, of which waited for: 3 -> 1; matrix products, arithmetic and copies ran while one was open for 0% -> 0% of each run, Pallas kernels for 22% -> 28%
where the time goes in v2:
time: 61.3 us; the launch traced here: 61.1 us
  Pallas kernels  47.3 us (77%)
  starting transfers between devices  7.7 us (13%)
  waiting for transfers between devices  5.64 us (9%)
    pallas_call x9, Pallas kernels, call(): pl.pallas_call(kernel, name=name, in_specs=[SMEM if n < smem else HBM if...  47.3 us
    ppermute x2, waiting for transfers between devices, exchange(): got_b = lax.ppermute(b, 'curve', pairs) if pairs else got_a  5.63 us
    ppermute x2, starting transfers between devices, exchange(): got_b = lax.ppermute(b, 'curve', pairs) if pairs else got_a  4.49 us
    ppermute x3, starting transfers between devices, exchange(): got_a = lax.ppermute(a, 'curve', swap_pairs(devices, levels, axis, 0))  3.21 us
  transfers between devices with their start and end apart: 5, of which 1 were waited for; matrix products, arithmetic and copies ran while one was open for 0% of the time, Pallas kernels for 28%

profile of v2, /device:TPU:24, one launch (start us, length us, event | category | flops | bytes accessed | tf_op | source)
XLA Modules:
  0.0 61.1 jit_solution(5513680574622238531)
XLA Ops:
  0.0 0.1 pad_add_fusion.par
  0.1 2.7 %prep.1 = (bf16[8,160,128]{2,1,0:T(8,128)(2,1)S(1)}, bf16[160,128]{1,0:T(8,128)(2,1)S(1)}, bf16[2,160,128]{2,1,0:T(8,128)(2,1)S(1)}, bf16[2,160,128]{2,1,0:T(8,128)(2,1)S(1)}) custom-call(s32[3]{0:T(128)S(1)} %pad_add_fusion.par, bf16[152,1024]{1,0:T(8,128)(2,1)} %mult_hbm.1, bf16[8,152,152]{2,1,0:T(8,128)(2,1)} %up_hbm.1, ...), custom_call_target="tpu_custom_call" | custom-call | flops 1000000000 | bytes 2097152 | tf_op jit(solution)/shard_map/prep/pallas_call | solution.py:691
  2.8 0.1 collective-permute-start
  2.8 2.4 %collective-permute-start.1 = (bf16[2,160,128]{2,1,0:T(8,128)(2,1)S(1)}, bf16[2,160,128]{2,1,0:T(8,128)(2,1)S(1)}, u32[]{:S(2)}, u32[]{:S(2)}) collective-permute-start(bf16[2,160,128]{2,1,0:T(8,128)(2,1)S(1)} %get-tuple-element.36), channel_id=1, source_target_pairs={{1,8},{8,1},{3,10},{10,3},{5,12},{12,5},{7,14},{14,7},{17,24},{24,... | collective-permute-start | bytes 245768 | tf_op jit(solution)/shard_map/ppermute | solution.py:725
  5.3 0.0 copy-start
  5.3 4.0 %main_operators.2.refs_0_ = bf16[316,152,128]{2,1,0:T(8,128)(2,1)S(1)} custom-call(bf16[152,152,316]{2,1,0:T(8,128)(2,1)} %bitcast.4), custom_call_target="tpu_custom_call" | custom-call | flops 1750000000 | bytes 7340032 | tf_op jit(solution)/shard_map/main_operators/pallas_call | solution.py:691
  9.3 0.0 collective-permute-done.got_a
  9.3 0.0 collective-permute-done.1.got_b
  9.3 0.0 copy-done
  9.3 1.0 %pack_y.1 = (bf16[8,160,128]{2,1,0:T(8,128)(2,1)S(1)}, bf16[160,128]{1,0:T(8,128)(2,1)S(1)}, bf16[5,160,128]{2,1,0:T(8,128)(2,1)S(1)}, bf16[5,160,128]{2,1,0:T(8,128)(2,1)S(1)}) custom-call(s32[3]{0:T(128)S(1)} %pad_add_fusion.par, bf16[8,160,128]{2,1,0:T(8,128)(2,1)S(1)} %get-tuple-element.33.own, bf16[160,128]{1,0:T(8,128)(2,1)S(1)} %get-tuple-element.34.coarse, ...), custom_call_target="tpu_custom_call" | custom-call | flops 1000000 | bytes 2097152 | tf_op jit(solution)/shard_map/pack_y/pallas_call | solution.py:691
  10.3 1.6 %collective-permute-start.2 = (bf16[5,160,128]{2,1,0:T(8,128)(2,1)S(1)}, bf16[5,160,128]{2,1,0:T(8,128)(2,1)S(1)}, u32[]{:S(2)}, u32[]{:S(2)}) collective-permute-start(bf16[5,160,128]{2,1,0:T(8,128)(2,1)S(1)} %get-tuple-element.41), channel_id=1, source_target_pairs={{0,2},{2,0},{1,3},{3,1},{4,6},{6,4},{5,7},{7,5},{8,10},{10,8},{9,1... | collective-permute-start | bytes 614408 | tf_op jit(solution)/shard_map/ppermute | solution.py:723
  11.9 0.0 copy-start.1
  11.9 2.0 %collective-permute-start.3 = (bf16[5,160,128]{2,1,0:T(8,128)(2,1)S(1)}, bf16[5,160,128]{2,1,0:T(8,128)(2,1)S(1)}, u32[]{:S(2)}, u32[]{:S(2)}) collective-permute-start(bf16[5,160,128]{2,1,0:T(8,128)(2,1)S(1)} %get-tuple-element.42), channel_id=1, source_target_pairs={{2,16},{16,2},{3,17},{17,3},{6,20},{20,6},{7,21},{21,7},{10,24},{2... | collective-permute-start | bytes 614408 | tf_op jit(solution)/shard_map/ppermute | solution.py:725
  13.9 5.9 %main_operators.3.main = bf16[316,152,128]{2,1,0:T(8,128)(2,1)S(1)} custom-call(bf16[152,152,316]{2,1,0:T(8,128)(2,1)} %bitcast.5, bf16[316,152,128]{2,1,0:T(8,128)(2,1)S(1)} %main_operators.2.refs_0_), custom_call_target="tpu_custom_call", output_to_operand_aliasing={{}: (1, {})} | custom-call | flops 3000000000 | bytes 12582912 | tf_op jit(solution)/shard_map/main_operators/pallas_call | solution.py:691
  19.9 0.0 collective-permute-done.2.got_a
  19.9 5.6 %collective-permute-done.3.got_b = bf16[5,160,128]{2,1,0:T(8,128)(2,1)S(1)} collective-permute-done((bf16[5,160,128]{2,1,0:T(8,128)(2,1)S(1)}, bf16[5,160,128]{2,1,0:T(8,128)(2,1)S(1)}, u32[]{:S(2)}, u32[]{:S(2)}) %collective-permute-start.3) | collective-permute-done | bytes 204832 | tf_op jit(solution)/shard_map/ppermute | solution.py:725
  25.5 1.1 %pack_x.1 = (bf16[8,160,128]{2,1,0:T(8,128)(2,1)S(1)}, bf16[8,160,128]{2,1,0:T(8,128)(2,1)S(1)}, bf16[160,128]{1,0:T(8,128)(2,1)S(1)}, bf16[160,128]{1,0:T(8,128)(2,1)S(1)}, bf16[7,160,128]{2,1,0:T(8,128)(2,1)S(1)}) custom-call(s32[3]{0:T(128)S(1)} %pad_add_fusion.par, bf16[8,160,128]{2,1,0:T(8,128)(2,1)S(1)} %get-tuple-element.33.own, ...), custom_call_target="tpu_custom_call" | custom-call | flops 1000000 | bytes 2097152 | tf_op jit(solution)/shard_map/pack_x/pallas_call | solution.py:691
  26.6 0.0 copy-start.2
  26.6 0.0 copy-start.6
  26.6 0.0 copy-start.3
  26.6 0.0 copy-start.4
  26.6 0.0 copy-start.5
  26.6 0.0 copy-start.7
  26.6 0.0 copy-start.8
  26.7 0.0 copy-start.9
  26.7 1.6 %collective-permute-start.4 = (bf16[7,160,128]{2,1,0:T(8,128)(2,1)S(1)}, bf16[7,160,128]{2,1,0:T(8,128)(2,1)S(1)}, u32[]{:S(2)}, u32[]{:S(2)}) collective-permute-start(bf16[7,160,128]{2,1,0:T(8,128)(2,1)S(1)} %get-tuple-element.48), channel_id=1, source_target_pairs={{0,4},{4,0},{1,5},{5,1},{2,6},{6,2},{3,7},{7,3},{8,12},{12,8},{9,1... | collective-permute-start | bytes 860168 | tf_op jit(solution)/shard_map/ppermute | solution.py:723
  28.3 0.0 copy-done.1
  28.3 4.2 %rest_operators.1.rest = bf16[112,152,128]{2,1,0:T(8,128)(2,1)S(1)} custom-call(bf16[152,152,316]{2,1,0:T(8,128)(2,1)} %bitcast.6, bf16[316,512]{1,0:T(8,128)(2,1)S(1)} %copy-done.1), custom_call_target="tpu_custom_call" | custom-call | flops 5000000000 | bytes 5242880 | tf_op jit(solution)/shard_map/rest_operators/pallas_call | solution.py:691
  32.4 0.0 copy-done.2
  32.4 0.0 copy-done.6
  32.4 0.5 masks.1.keep
  33.0 2.3 %early.1 = (bf16[216,160,128]{2,1,0:T(8,128)(2,1)S(1)}, bf16[49,160,256]{2,1,0:T(8,128)(2,1)S(1)}) custom-call(bf16[8,160,128]{2,1,0:T(8,128)(2,1)S(1)} %get-tuple-element.33.own, bf16[8,160,128]{2,1,0:T(8,128)(2,1)S(1)} %get-tuple-element.39.hz, bf16[8,160,128]{2,1,0:T(8,128)(2,1)S(1)} %get-tuple-element.46.hy, ...), custom_call_target="tpu_custom_call" | custom-call | flops 1000000000 | bytes 8388608 | tf_op jit(solution)/shard_map/early/pallas_call | solution.py:691
  35.2 0.0 collective-permute-done.4.got_a.got_b
  35.2 0.0 copy-done.3
  35.2 0.0 copy-done.4
  35.3 0.0 copy-done.5
  35.3 0.0 copy-done.7
  35.3 0.0 copy-done.8
  35.3 0.0 copy-done.9
  35.3 25.8 %translate.1 = (bf16[152,1024]{1,0:T(8,128)(2,1)}, bf16[216,160,128]{2,1,0:T(8,128)(2,1)S(1)}, bf16[49,160,256]{2,1,0:T(8,128)(2,1)S(1)}) custom-call(s32[3]{0:T(128)S(1)} %pad_add_fusion.par, s32[2536]{0:T(1024)S(1)} %copy-done.9, s32[2513]{0:T(1024)S(1)} %copy-done.8, ...), custom_call_target="tpu_custom_call", output_to_operand_aliasing={{1}: (18, {}), {2}: (19, {})} | custom-call | flops 20000000000 | bytes 20971520 | tf_op jit(solution)/shard_map/translate/pallas_call | solution.py:691
Async XLA Ops:
  2.8 6.5 %collective-permute-start = (bf16[2,160,128]{2,1,0:T(8,128)(2,1)S(1)}, bf16[2,160,128]{2,1,0:T(8,128)(2,1)S(1)}, u32[]{:S(2)}, u32[]{:S(2)}) collective-permute-start(bf16[2,160,128]{2,1,0:T(8,128)(2,1)S(1)} %get-tuple-element.35), channel_id=1, source_target_pairs={{0,1},{1,0},{2,3},{3,2},{4,5},{5,4},{6,7},{7,6},{8,9},{9,8},{10,11... | collective-permute-start | bytes 245768 | tf_op jit(solution)/shard_map/ppermute | solution.py:723
  2.8 6.5 %collective-permute-start.1 = (bf16[2,160,128]{2,1,0:T(8,128)(2,1)S(1)}, bf16[2,160,128]{2,1,0:T(8,128)(2,1)S(1)}, u32[]{:S(2)}, u32[]{:S(2)}) collective-permute-start(bf16[2,160,128]{2,1,0:T(8,128)(2,1)S(1)} %get-tuple-element.36), channel_id=1, source_target_pairs={{1,8},{8,1},{3,10},{10,3},{5,12},{12,5},{7,14},{14,7},{17,24},{24,... | collective-permute-start | bytes 245768 | tf_op jit(solution)/shard_map/ppermute | solution.py:725
  5.3 4.0 %copy-start = (f32[179,128]{1,0:T(8,128)S(1)}, f32[179,128]{1,0:T(8,128)}, u32[]{:S(2)}) copy-start(f32[179,128]{1,0:T(8,128)} %constant.23.clone.tab_hbm.tab) | copy-start | bytes 274948
  10.3 9.5 %collective-permute-start.2 = (bf16[5,160,128]{2,1,0:T(8,128)(2,1)S(1)}, bf16[5,160,128]{2,1,0:T(8,128)(2,1)S(1)}, u32[]{:S(2)}, u32[]{:S(2)}) collective-permute-start(bf16[5,160,128]{2,1,0:T(8,128)(2,1)S(1)} %get-tuple-element.41), channel_id=1, source_target_pairs={{0,2},{2,0},{1,3},{3,1},{4,6},{6,4},{5,7},{7,5},{8,10},{10,8},{9,1... | collective-permute-start | bytes 614408 | tf_op jit(solution)/shard_map/ppermute | solution.py:723
  11.9 16.4 %copy-start.1 = (bf16[316,512]{1,0:T(8,128)(2,1)S(1)}, bf16[316,512]{1,0:T(8,128)(2,1)}, u32[]{:S(2)}) copy-start(bf16[316,512]{1,0:T(8,128)(2,1)} %constant.24.clone.order) | copy-start | bytes 970756
  11.9 13.6 %collective-permute-start.3 = (bf16[5,160,128]{2,1,0:T(8,128)(2,1)S(1)}, bf16[5,160,128]{2,1,0:T(8,128)(2,1)S(1)}, u32[]{:S(2)}, u32[]{:S(2)}) collective-permute-start(bf16[5,160,128]{2,1,0:T(8,128)(2,1)S(1)} %get-tuple-element.42), channel_id=1, source_target_pairs={{2,16},{16,2},{3,17},{17,3},{6,20},{20,6},{7,21},{21,7},{10,24},{2... | collective-permute-start | bytes 614408 | tf_op jit(solution)/shard_map/ppermute | solution.py:725
  26.6 5.9 %copy-start.2 = (s32[316,1024]{1,0:T(8,128)S(1)}, s32[316,1024]{1,0:T(8,128)}, u32[]{:S(2)}) copy-start(s32[316,1024]{1,0:T(8,128)} %fine.1) | copy-start | bytes 3883012
  26.6 5.8 %copy-start.6 = (bf16[512,512]{1,0:T(8,128)(2,1)S(1)}, bf16[512,512]{1,0:T(8,128)(2,1)}, u32[]{:S(2)}) copy-start(bf16[512,512]{1,0:T(8,128)(2,1)} %constant.22.clone.hot_hbm.hot) | copy-start | bytes 1572868
  26.6 8.6 %copy-start.3 = (bf16[8,152,152]{2,1,0:T(8,128)(2,1)S(1)}, bf16[8,152,152]{2,1,0:T(8,128)(2,1)}, u32[]{:S(2)}) copy-start(bf16[8,152,152]{2,1,0:T(8,128)(2,1)} %down.1) | copy-start | bytes 1108996
  26.6 8.6 %copy-start.4 = (s32[316,128]{1,0:T(8,128)S(1)}, s32[316,128]{1,0:T(8,128)}, u32[]{:S(2)}) copy-start(s32[316,128]{1,0:T(8,128)} %clist.1) | copy-start | bytes 485380
  26.6 8.6 %copy-start.5 = (bf16[152,152]{1,0:T(8,128)(2,1)S(1)}, bf16[152,152]{1,0:T(8,128)(2,1)}, u32[]{:S(2)}) copy-start(bf16[152,152]{1,0:T(8,128)(2,1)} %inverse.1) | copy-start | bytes 138628
  26.6 8.6 %copy-start.7 = (f32[320,128]{1,0:T(8,128)S(1)}, f32[320,128]{1,0:T(8,128)}, u32[]{:S(2)}) copy-start(f32[320,128]{1,0:T(8,128)} %constant.26.clone.outside) | copy-start | bytes 491524
  26.6 8.6 %copy-start.8 = (s32[2513]{0:T(1024)S(1)}, s32[2513]{0:T(1024)}, u32[]{:S(2)}) copy-start(s32[2513]{0:T(1024)} %constant.27.clone.ct) | copy-start | bytes 30160
  26.7 8.6 %copy-start.9 = (s32[2536]{0:T(1024)S(1)}, s32[2536]{0:T(1024)}, u32[]{:S(2)}) copy-start(s32[2536]{0:T(1024)} %constant.25.clone.ft) | copy-start | bytes 30436
  26.7 8.6 %collective-permute-start.4 = (bf16[7,160,128]{2,1,0:T(8,128)(2,1)S(1)}, bf16[7,160,128]{2,1,0:T(8,128)(2,1)S(1)}, u32[]{:S(2)}, u32[]{:S(2)}) collective-permute-start(bf16[7,160,128]{2,1,0:T(8,128)(2,1)S(1)} %get-tuple-element.48), channel_id=1, source_target_pairs={{0,4},{4,0},{1,5},{5,1},{2,6},{6,2},{3,7},{7,3},{8,12},{12,8},{9,1... | collective-permute-start | bytes 860168 | tf_op jit(solution)/shard_map/ppermute | solution.py:723

commit v3 on v2

--- a/solution.py
+++ b/solution.py
@@ -116,12 +116,8 @@
     for s in range(8):
         masks.add(("zpack", s), {l for l in every if l % PZ == s})
     row = PY * PZ
-    low_z = {lane_of((i, 0, k)) for i in range(PX) for k in (-1, PZ)}
-    up_z = {lane_of((i, PY - 1, k)) for i in range(PX) for k in (-1, PZ)}
-    masks.add(("ysrc", 0), low_z)
-    masks.add(("ysrc", 1), up_z)
-    for t in range(3):
-        masks.add(("ypack", t), {l for l in every if (l % row) // 10 == t})
+    for t in range(PY):
+        masks.add(("ypack", t), {l for l in every if l // PZ % PY == t})
     masks.add(("xsrc_a", 0), set(range(row)))
     masks.add(("xsrc_a", 1), set(range(LANES - row, LANES)))
     for side, i in ((0, 0), (1, PX - 1)):
@@ -170,12 +166,12 @@
 
 
 def octant_order():
-    row = np.arange(PX * BY * BZ)
+    size = PX * BY * BZ
+    row = lax.broadcasted_iota(jnp.int32, (size, 1), 0)
+    column = lax.broadcasted_iota(jnp.int32, (size, size), 1)
     i, y, z = row // (BY * BZ), row // BZ % BY, row % BZ
-    column = (2 * (y % 2) + z % 2) * LANES + i * PY * PZ + (y // 2) * PZ + z // 2
-    hot = np.zeros((len(row), len(row)), np.float32)
-    hot[row, column] = 1
-    return hot
+    place = (2 * (y % 2) + z % 2) * LANES + i * PY * PZ + (y // 2) * PZ + z // 2
+    return jnp.where(column == place, 1.0, 0.0).astype(BF)
 
 
 def to_octants(x, hot):
@@ -190,40 +186,44 @@
 
 
 def prep_kernel(
-    par, mult_hbm, up_hbm, hot_hbm, tab_hbm, own, coarse, send_a, send_b, mult, up, hot, tab, sems
+    par, mult_hbm, up_hbm, tab_hbm, own, coarse, send_a, send_b, hot, mult, up, tab, sems
 ):
     copies = [
         pltpu.make_async_copy(src, dst, sems.at[n])
         for n, (src, dst) in enumerate(
-            ((mult_hbm, mult), (hot_hbm, hot), (up_hbm, up), (tab_hbm, tab))
+            ((mult_hbm, mult), (tab_hbm, tab), (up_hbm, up))
         )
     ]
     for copy in copies:
         copy.start()
     chans = mult.shape[0]
     rows = own.shape[1]
+    hot[...] = octant_order()
     copies[0].wait()
     copies[1].wait()
     halves = to_octants(mult[...], hot[...])
     copies[2].wait()
-    copies[3].wait()
     total = jnp.zeros((chans, LANES), F32)
-    pack = [None, None]
+    pack = [[None] * 2, [None] * 2]
     for s in range(8):
         x = halves[s // 4][:, (s % 4) * LANES : (s % 4 + 1) * LANES].astype(BF)
         total = total + jnp.dot(up[s], x, preferred_element_type=F32)
         x = padded(x, rows)
         own[s] = x
+        block, t = s // PY, s % PY
         for side in range(2):
-            moved = roll(x, s - (PZ - 1) * side)
-            pack[side] = moved if s == 0 else pick(tab, ("zpack", s), moved, pack[side])
+            moved = roll(x, PZ * (t - (PY - 1) * side))
+            pack[side][block] = (
+                moved if t == 0 else pick(tab, ("ypack", t), moved, pack[side][block])
+            )
     c = padded(total.astype(BF), rows)
     coarse[...] = c
-    even = par[2] == 0
-    send_a[0] = jnp.where(even, pack[1], pack[0])
-    send_b[0] = jnp.where(even, pack[0], pack[1])
-    send_a[1] = c
-    send_b[1] = c
+    even = par[1] == 0
+    for block in range(2):
+        send_a[block] = jnp.where(even, pack[1][block], pack[0][block])
+        send_b[block] = jnp.where(even, pack[0][block], pack[1][block])
+    send_a[2] = c
+    send_b[2] = c
 
 
 def sides(par, axis, got_a, got_b):
@@ -233,48 +233,41 @@
     return plus, minus
 
 
-def y_kernel(par, own, coarse, got_a, got_b, tab, hz, cz, send_a, send_b):
-    p, m = sides(par, 2, got_a[0], got_b[0])
-    for s in range(8):
-        hz[s] = pick(
-            tab, ("plus", 1, (0, 0, 1), 2), roll(p, PZ - s), roll(m, -1 - s)
-        )
-    p, m = sides(par, 2, got_a[1], got_b[1])
-    far = pick(tab, ("plus", 2, (0, 0, 1), 2), roll(p, PZ), roll(m, -PZ))
-    cz[...] = far
-    even = par[1] == 0
-    pack = [[None] * 3, [None] * 3]
-    for s in range(8):
-        block, t = s // 3, s % 3
-        for side in range(2):
-            src = pick(tab, ("ysrc", side), hz[s], own[s])
-            moved = roll(src, 1 + 10 * t - (PY - 1) * PZ * side)
-            pack[side][block] = (
-                moved if t == 0 else pick(tab, ("ypack", t), moved, pack[side][block])
-            )
-    for block in range(3):
-        send_a[block] = jnp.where(even, pack[1][block], pack[0][block])
-        send_b[block] = jnp.where(even, pack[0][block], pack[1][block])
-    for send in (send_a, send_b):
-        send[3] = coarse[...]
-        send[4] = far
-
-
-def x_kernel(par, own, coarse, hz, cz, got_a, got_b, tab, hy, hyz, cy, cyz, *sends):
+def z_kernel(par, own, coarse, got_a, got_b, tab, hy, cy, send_a, send_b):
     row = PY * PZ
     for s in range(8):
-        block, t = s // 3, s % 3
+        block, t = s // PY, s % PY
         p, m = sides(par, 1, got_a[block], got_b[block])
-        p = roll(p, row - 1 - 10 * t)
-        m = roll(m, -PZ - 1 - 10 * t)
-        hy[s] = pick(tab, ("plus", 1, (0, 1, 0), 1), p, m)
-        hyz[s] = pick(tab, ("plus", 1, (0, 1, 1), 1), p, m)
-    near = []
-    for n, kind in ((3, (0, 1, 0)), (4, (0, 1, 1))):
-        p, m = sides(par, 1, got_a[n], got_b[n])
-        near.append(pick(tab, ("plus", 2, kind, 1), roll(p, row), roll(m, -row)))
-    cy[...] = near[0]
-    cyz[...] = near[1]
+        hy[s] = pick(
+            tab, ("plus", 1, (0, 1, 0), 1), roll(p, row - PZ * t), roll(m, -PZ - PZ * t)
+        )
+    p, m = sides(par, 1, got_a[2], got_b[2])
+    far = pick(tab, ("plus", 2, (0, 1, 0), 1), roll(p, row), roll(m, -row))
+    cy[...] = far
+    even = par[2] == 0
+    for n, ref in ((0, own), (1, hy)):
+        pack = [None, None]
+        for s in range(8):
+            for side in range(2):
+                moved = roll(ref[s], s - (PZ - 1) * side)
+                pack[side] = moved if s == 0 else pick(tab, ("zpack", s), moved, pack[side])
+        send_a[n] = jnp.where(even, pack[1], pack[0])
+        send_b[n] = jnp.where(even, pack[0], pack[1])
+    for send in (send_a, send_b):
+        send[2] = coarse[...]
+        send[3] = far
+
+
+def x_kernel(par, own, coarse, hy, cy, got_a, got_b, tab, hz, hyz, cz, cyz, *sends):
+    row = PY * PZ
+    for n, ref, kind in ((0, hz, (0, 0, 1)), (1, hyz, (0, 1, 1))):
+        p, m = sides(par, 2, got_a[n], got_b[n])
+        for s in range(8):
+            ref[s] = pick(tab, ("plus", 1, kind, 2), roll(p, PZ - s), roll(m, -1 - s))
+    for n, ref, kind in ((2, cz, (0, 0, 1)), (3, cyz, (0, 1, 1))):
+        p, m = sides(par, 2, got_a[n], got_b[n])
+        ref[...] = pick(tab, ("plus", 2, kind, 2), roll(p, PZ), roll(m, -PZ))
+    near = [cy[...], cyz[...]]
     half = LANES // 2
     other = roll(near[0], half)
     low = pick(tab, "half", coarse[...], pick(tab, ("cy", 0), near[0], other))
@@ -389,62 +382,6 @@
     return 4 * o[0] + 2 * o[1] + o[2]
 
 
-def fine_table():
-    rows, shape = [], None
-    for j in range(4):
-        row, form = [], []
-        for fours, first, second in jobs_of(j):
-            row += [octant_number(first), octant_number(second)]
-            counts = []
-            for f in fours:
-                row.append(f)
-                counts.append(len(FOURS[f]))
-                for d in FOURS[f]:
-                    row += [NUMBER[d], slot_of(first, d), slot_of(second, d)]
-            form.append(counts)
-        assert shape is None or shape == form
-        rows.append(row)
-        shape = form
-    return np.array(rows, np.int32), shape
-
-
-FINE_TABLE, FINE_FORM = fine_table()
-
-
-def coarse_table(spare):
-    chunks = []
-    for turn in range(PX):
-        offsets = [d for d in SHIFTS if d[0] % PX == turn]
-        fours = [n for n, four in enumerate(FOURS) if four[0][0] % PX == turn]
-        parts = 1 if turn == 0 else 2
-        cut, cut4 = -(-len(offsets) // parts), -(-len(fours) // parts)
-        for part in range(parts):
-            chunks.append(
-                (turn, offsets[part * cut : (part + 1) * cut], fours[part * cut4 : (part + 1) * cut4])
-            )
-    count = max(len(c[1]) for c in chunks)
-    count4 = max(len(c[2]) for c in chunks)
-    count += (count + count4) % 2
-
-    def entry(d):
-        if d is None:
-            return [0, spare, 24]
-        return [NUMBER[d], NUMBER[d], (d[1] + 3) * 7 + d[2] + 3]
-
-    rows = []
-    for turn, offsets, fours in chunks:
-        row = [turn]
-        for n in range(count):
-            row += entry(offsets[n] if n < len(offsets) else None)
-        for n in range(count4):
-            four = FOURS[fours[n]] if n < len(fours) else ()
-            row.append(fours[n] if n < len(fours) else 0)
-            for place in range(4):
-                row += entry(four[place] if place < len(four) else None)
-        rows.append(row)
-    return np.array(rows, np.int32), count, count4
-
-
 def rest_order(offsets):
     hot = np.zeros((offsets, 4 * LANES), np.float32)
     for n, four in enumerate(FOURS):
@@ -531,8 +468,11 @@
     return jnp.dot(left, right, preferred_element_type=F32)
 
 
+GROUP = 24
+
+
 def main_kernel(
-    form, par, ft, ct, own, hz, hy, hyz, got_a, got_b, tab, outside, main, rest, keep, clist,
+    lone, par, own, hz, hy, hyz, got_a, got_b, tab, outside, main, rest, keep, clist,
     down, inverse, hot, _slots, _plane, out, slots, plane, acc, cacc, cmask,
 ):
     chans = acc.shape[1]
@@ -567,7 +507,7 @@
         far = (PX - 1) * row
 
         at_a, at_b = -8 - 64 * t, -9 - 2 * u - 64 * v
-        if form[3]:
+        if lone:
             hx = hxy = turn_by(got_a[block], at_a + far * par[0])
             hxz = hxyz = turn_by(got_a[4], at_b + far * par[0])
         else:
@@ -586,47 +526,39 @@
         steps = [d for d in itertools.product((-1, 0, 1), repeat=3) if d[0]]
         put_slots(tab, s, kinds, slots, steps)
 
-    def coarse_chunk(c):
-        base = c * form[2]
-        turn = ct[base]
-
-        def source(at, lo, hi):
-            md, pn = ct[at + 1], ct[at + 2]
-            shape = (hi - lo, 2 * LANES)
-            mask = jnp.broadcast_to(cmask[turn, pl.ds(md, 1), :], shape).astype(BF)
-            return plane[pn, lo:hi] * mask
-
-        at = base + 1
-        pieces = []
-        for n in range(form[0]):
-            pieces.append((main[ct[at]], source(at, 0, LANES)))
-            at = at + 3
-        for n in range(form[1]):
-            four = ct[at]
-            at = at + 1
-            rests = []
-            for place in range(4):
-                rests.append(source(at, LANES, rows))
-                at = at + 3
-            pieces.append((rest[four], jnp.concatenate(rests, 0)))
-        cacc[turn] += dot_pieces(pieces)
-
-    chunks = ct.shape[0] // form[2]
-    for s in range(chunks, 8):
-        fine_sources(s)
-
-    def both(n, carry):
-        fine_sources(n)
-        coarse_chunk(n)
-        return carry
-
-    lax.fori_loop(0, chunks, both, 0)
-
-    def fine_body(j, carry):
-        at = j * FINE_TABLE.shape[1]
-        for counts in FINE_FORM:
-            first_o, second_o = ft[at], ft[at + 1]
-            at = at + 2
+    def source(d, lo, hi):
+        n = NUMBER[d]
+        mask = jnp.broadcast_to(cmask[d[0] % PX, n : n + 1, :], (hi - lo, 2 * LANES)).astype(BF)
+        return plane[(d[1] + 3) * 7 + d[2] + 3, lo:hi] * mask
+
+    def whole(d):
+        return main[NUMBER[d]], source(d, 0, LANES)
+
+    def quarters(n):
+        parts = [source(d, LANES, rows) for d in FOURS[n]]
+        if len(parts) < 4:
+            parts.append(jnp.zeros((32 * (4 - len(parts)), 2 * LANES), BF))
+        return rest[n], jnp.concatenate(parts, 0)
+
+    groups = []
+    for turn in range(PX):
+        makers = [functools.partial(whole, d) for d in SHIFTS if d[0] % PX == turn]
+        makers += [
+            functools.partial(quarters, n) for n, four in enumerate(FOURS) if four[0][0] % PX == turn
+        ]
+        parts = -(-len(makers) // GROUP)
+        size = -(-len(makers) // (2 * parts)) * 2
+        groups += [(turn, makers[n : n + size]) for n in range(0, len(makers), size)]
+    done = 0
+    for n, (turn, makers) in enumerate(groups):
+        while done < 8 and done * len(groups) <= 8 * n:
+            fine_sources(done)
+            done += 1
+        cacc[turn] += dot_pieces([make() for make in makers])
+
+    for j in range(4):
+        for fours, first, second in jobs_of(j):
+            first_o, second_o = octant_number(first), octant_number(second)
             pieces = []
 
             def flush(part):
@@ -634,31 +566,25 @@
                 acc[first_o] += got[:, 0:LANES]
                 acc[second_o] += got[:, LANES:]
 
-            for count in counts:
-                four = ft[at]
-                at = at + 1
+            for four in fours:
                 rests = []
-                for n in range(count):
-                    d, one, two = ft[at], ft[at + 1], ft[at + 2]
-                    at = at + 3
+                for d in FOURS[four]:
+                    n = NUMBER[d]
                     x = []
-                    for slot, o in ((one, first_o), (two, second_o)):
-                        mask = jnp.broadcast_to(keep[o, pl.ds(d, 1), :], (rows, LANES)).astype(BF)
-                        x.append(slots[slot] * mask)
+                    for octant, o in ((first, first_o), (second, second_o)):
+                        mask = jnp.broadcast_to(keep[o, n : n + 1, :], (rows, LANES)).astype(BF)
+                        x.append(slots[slot_of(octant, d)] * mask)
                     x = jnp.concatenate(x, 1)
-                    pieces.append((main[d], x[0:LANES]))
+                    pieces.append((main[n], x[0:LANES]))
                     rests.append(x[LANES:rows])
-                if count < 4:
-                    rests.append(jnp.zeros((32 * (4 - count), 2 * LANES), BF))
+                if len(rests) < 4:
+                    rests.append(jnp.zeros((32 * (4 - len(rests)), 2 * LANES), BF))
                 pieces.append((rest[four], jnp.concatenate(rests, 0)))
-                while len(pieces) >= 20:
-                    flush(pieces[:20])
-                    pieces = pieces[20:]
+                while len(pieces) >= GROUP:
+                    flush(pieces[:GROUP])
+                    pieces = pieces[GROUP:]
             if pieces:
                 flush(pieces)
-        return carry
-
-    lax.fori_loop(0, 4, fine_body, 0)
     check = jnp.zeros(cacc.shape[1:2] + (LANES,), F32)
     for turn in range(PX):
         check = check + roll(cacc[turn, :, 0:LANES] + cacc[turn, :, LANES:], -turn * row)
@@ -715,7 +641,6 @@
     limits = grid_counts(levels)
     position = lax.axis_index("curve")
     par = jnp.stack([position >> (2 - axis) & 1 for axis in range(3)]).astype(jnp.int32)
-    hot = jnp.asarray(octant_order(), BF)
     tab = jnp.asarray(TABLE)
     row_pad = (offsets + 8) // 8 * 8
 
@@ -727,19 +652,19 @@
 
     full = ((8, rows, LANES), BF)
     one = ((rows, LANES), BF)
-    own, coarse, a, b = call(
-        prep_kernel, "prep", 1, (par, multipole, upward_maps, hot, tab),
-        [full, one, ((2, rows, LANES), BF), ((2, rows, LANES), BF)], 16 * MIB,
-        flops=10**9, bytes_=2 * MIB, hbm=(1, 2, 3, 4),
+    side = PX * BY * BZ
+    own, coarse, a, b, hot = call(
+        prep_kernel, "prep", 1, (par, multipole, upward_maps, tab),
+        [full, one, ((3, rows, LANES), BF), ((3, rows, LANES), BF), ((side, side), BF)], 16 * MIB,
+        flops=10**9, bytes_=2 * MIB, hbm=(1, 2, 3),
         scratch=[
             pltpu.VMEM(multipole.shape, BF),
             pltpu.VMEM(upward_maps.shape, BF),
-            pltpu.VMEM(hot.shape, BF),
             pltpu.VMEM(tab.shape, F32),
-            pltpu.SemaphoreType.DMA((4,)),
+            pltpu.SemaphoreType.DMA((3,)),
         ],
     )
-    za, zb = exchange(2, a, b)
+    ya, yb = exchange(1, a, b)
     rests = (len(FOURS) + 7) // 8 * 8
     turned = jnp.transpose(transfer_maps, (1, 2, 0))
     order = jnp.asarray(rest_order(offsets), BF)
@@ -756,20 +681,20 @@
         )
         return main
 
-    ready = 2 * blocks // 5
+    ready = 3 * blocks // 5
     main = turn(0, ready)
-    za, zb, main = lax.optimization_barrier((za, zb, main))
-    hz, cz, a, b = call(
-        y_kernel, "pack_y", 1, (par, own, coarse, za, zb, tab),
-        [full, one, ((5, rows, LANES), BF), ((5, rows, LANES), BF)], 16 * MIB,
+    ya, yb, main = lax.optimization_barrier((ya, yb, main))
+    hy, cy, a, b = call(
+        z_kernel, "pack_z", 1, (par, own, coarse, ya, yb, tab),
+        [full, one, ((4, rows, LANES), BF), ((4, rows, LANES), BF)], 16 * MIB,
         flops=10**6, bytes_=2 * MIB,
     )
-    ya, yb = exchange(1, a, b)
+    za, zb = exchange(2, a, b)
     main = turn(ready, blocks - ready, main)
-    ya, yb, main = lax.optimization_barrier((ya, yb, main))
+    za, zb, main = lax.optimization_barrier((za, zb, main))
     lone = not swap_pairs(devices, levels, 0, 1)
-    hy, hyz, cy, cyz, *sends = call(
-        x_kernel, "pack_x", 1, (par, own, coarse, hz, cz, ya, yb, tab),
+    hz, hyz, cz, cyz, *sends = call(
+        x_kernel, "pack_x", 1, (par, own, coarse, hy, cy, za, zb, tab),
         [full, full, one, one] + [((7, rows, LANES), BF)] * (1 if lone else 2), 16 * MIB,
         flops=10**6, bytes_=2 * MIB,
     )
@@ -790,17 +715,14 @@
         flops=10**9, bytes_=2 * MIB,
     )
     xa, xb, slots, plane, keep, rest = lax.optimization_barrier((xa, xb, slots, plane, keep, rest))
-    ft = jnp.asarray(FINE_TABLE.reshape(-1))
-    table, count, count4 = coarse_table(row_pad - 1)
     beyond = [TABLE[MASKS.rows["stage", 2, 0, (0, 0, 0), d[0]]] for d in SHIFTS]
     outside = jnp.asarray(np.stack(beyond + [0 * beyond[0]] * (row_pad - offsets)))
-    ct = jnp.asarray(table.reshape(-1))
     out, _, _ = call(
-        functools.partial(main_kernel, (count, count4, table.shape[1], lone)), "translate", 3,
-        (par, ft, ct, own, hz, hy, hyz, xa, xb, tab, outside, main, rest, keep,
+        functools.partial(main_kernel, lone), "translate", 1,
+        (par, own, hz, hy, hyz, xa, xb, tab, outside, main, rest, keep,
          coarse_lists, downward_maps, check_inverse, hot, slots, plane),
         [((chans, multipole.shape[1]), BF), *early],
-        14 * MIB, aliases={18: 1, 19: 2},
+        14 * MIB, aliases={16: 1, 17: 2},
         scratch=[
             pltpu.VMEM((8, chans, LANES), F32),
             pltpu.VMEM((PX, chans, 2 * LANES), F32),

time: 61.3 us -> 54.9 us (0.90)
  the two profiles are of different devices: /device:TPU:24 before, /device:TPU:17 now
where the time goes in v3:
time: 54.9 us; the launch traced here: 54.7 us
  Pallas kernels  42.1 us (77%)
  starting transfers between devices  12.2 us (22%)
    pallas_call x9, Pallas kernels, call(): pl.pallas_call(kernel, name=name, in_specs=[SMEM if n < smem else HBM if...  42.1 us
    ppermute x2, starting transfers between devices, exchange(): got_b = lax.ppermute(b, 'curve', pairs) if pairs else got_a  7.57 us
    ppermute x3, starting transfers between devices, exchange(): got_a = lax.ppermute(a, 'curve', swap_pairs(devices, levels, axis, 0))  4.64 us
  transfers between devices with their start and end apart: 5, of which 0 were waited for; matrix products, arithmetic and copies ran while one was open for 0% of the time, Pallas kernels for 31%

profile of v3, /device:TPU:17, one launch (start us, length us, event | category | flops | bytes accessed | tf_op | source)
XLA Modules:
  0.0 54.7 jit_solution(6214783858077540555)
XLA Ops:
  0.0 0.1 pad_add_fusion.par
  0.1 2.5 %prep.1 = (bf16[8,160,128]{2,1,0:T(8,128)(2,1)S(1)}, bf16[160,128]{1,0:T(8,128)(2,1)S(1)}, bf16[3,160,128]{2,1,0:T(8,128)(2,1)S(1)}, bf16[3,160,128]{2,1,0:T(8,128)(2,1)S(1)}, bf16[512,512]{1,0:T(8,128)(2,1)S(1)}) custom-call(s32[3]{0:T(128)S(1)} %pad_add_fusion.par, bf16[152,1024]{1,0:T(8,128)(2,1)} %mult_hbm.1, bf16[8,152,152]{2,1,0:T(8,128)(2,1)} %up_hbm.1, ...), custom_call_target="tpu_custom_call" | custom-call | flops 1000000000 | bytes 2097152 | tf_op jit(solution)/shard_map/prep/pallas_call | solution.py:617
  2.6 1.3 %collective-permute-start = (bf16[3,160,128]{2,1,0:T(8,128)(2,1)S(1)}, bf16[3,160,128]{2,1,0:T(8,128)(2,1)S(1)}, u32[]{:S(2)}, u32[]{:S(2)}) collective-permute-start(bf16[3,160,128]{2,1,0:T(8,128)(2,1)S(1)} %get-tuple-element.36), channel_id=1, source_target_pairs={{0,2},{2,0},{1,3},{3,1},{4,6},{6,4},{5,7},{7,5},{8,10},{10,8},{9,1... | collective-permute-start | bytes 368648 | tf_op jit(solution)/shard_map/ppermute | solution.py:648
  3.9 1.9 %collective-permute-start.1 = (bf16[3,160,128]{2,1,0:T(8,128)(2,1)S(1)}, bf16[3,160,128]{2,1,0:T(8,128)(2,1)S(1)}, u32[]{:S(2)}, u32[]{:S(2)}) collective-permute-start(bf16[3,160,128]{2,1,0:T(8,128)(2,1)S(1)} %get-tuple-element.37), channel_id=1, source_target_pairs={{2,16},{16,2},{3,17},{17,3},{6,20},{20,6},{7,21},{21,7},{10,24},{2... | collective-permute-start | bytes 368648 | tf_op jit(solution)/shard_map/ppermute | solution.py:650
  5.8 0.0 copy-start
  5.8 5.5 %main_operators.2.refs_0_ = bf16[316,152,128]{2,1,0:T(8,128)(2,1)S(1)} custom-call(bf16[152,152,316]{2,1,0:T(8,128)(2,1)} %bitcast.4), custom_call_target="tpu_custom_call" | custom-call | flops 2750000128 | bytes 11534336 | tf_op jit(solution)/shard_map/main_operators/pallas_call | solution.py:617
  11.4 0.0 collective-permute-done.got_a
  11.4 0.0 collective-permute-done.1.got_b
  11.4 0.0 copy-done
  11.4 1.1 %pack_z.1 = (bf16[8,160,128]{2,1,0:T(8,128)(2,1)S(1)}, bf16[160,128]{1,0:T(8,128)(2,1)S(1)}, bf16[4,160,128]{2,1,0:T(8,128)(2,1)S(1)}, bf16[4,160,128]{2,1,0:T(8,128)(2,1)S(1)}) custom-call(s32[3]{0:T(128)S(1)} %pad_add_fusion.par, bf16[8,160,128]{2,1,0:T(8,128)(2,1)S(1)} %get-tuple-element.34.own, bf16[160,128]{1,0:T(8,128)(2,1)S(1)} %get-tuple-element.35.coarse, ...), custom_call_target="tpu_custom_call" | custom-call | flops 1000000 | bytes 2097152 | tf_op jit(solution)/shard_map/pack_z/pallas_call | solution.py:617
  12.5 2.1 %collective-permute-start.2 = (bf16[4,160,128]{2,1,0:T(8,128)(2,1)S(1)}, bf16[4,160,128]{2,1,0:T(8,128)(2,1)S(1)}, u32[]{:S(2)}, u32[]{:S(2)}) collective-permute-start(bf16[4,160,128]{2,1,0:T(8,128)(2,1)S(1)} %get-tuple-element.42), channel_id=1, source_target_pairs={{0,1},{1,0},{2,3},{3,2},{4,5},{5,4},{6,7},{7,6},{8,9},{9,8},{10,11... | collective-permute-start | bytes 491528 | tf_op jit(solution)/shard_map/ppermute | solution.py:648
  14.6 0.0 copy-start.1
  14.6 5.7 %collective-permute-start.3 = (bf16[4,160,128]{2,1,0:T(8,128)(2,1)S(1)}, bf16[4,160,128]{2,1,0:T(8,128)(2,1)S(1)}, u32[]{:S(2)}, u32[]{:S(2)}) collective-permute-start(bf16[4,160,128]{2,1,0:T(8,128)(2,1)S(1)} %get-tuple-element.43), channel_id=1, source_target_pairs={{1,8},{8,1},{3,10},{10,3},{5,12},{12,5},{7,14},{14,7},{17,24},{24,... | collective-permute-start | bytes 491528 | tf_op jit(solution)/shard_map/ppermute | solution.py:650
  20.2 4.3 %main_operators.3.main = bf16[316,152,128]{2,1,0:T(8,128)(2,1)S(1)} custom-call(bf16[152,152,316]{2,1,0:T(8,128)(2,1)} %bitcast.5, bf16[316,152,128]{2,1,0:T(8,128)(2,1)S(1)} %main_operators.2.refs_0_), custom_call_target="tpu_custom_call", output_to_operand_aliasing={{}: (1, {})} | custom-call | flops 2000000000 | bytes 8388608 | tf_op jit(solution)/shard_map/main_operators/pallas_call | solution.py:617
  24.6 0.0 collective-permute-done.2.got_a
  24.6 0.0 collective-permute-done.3.got_b
  24.6 1.3 %pack_x.1 = (bf16[8,160,128]{2,1,0:T(8,128)(2,1)S(1)}, bf16[8,160,128]{2,1,0:T(8,128)(2,1)S(1)}, bf16[160,128]{1,0:T(8,128)(2,1)S(1)}, bf16[160,128]{1,0:T(8,128)(2,1)S(1)}, bf16[7,160,128]{2,1,0:T(8,128)(2,1)S(1)}) custom-call(s32[3]{0:T(128)S(1)} %pad_add_fusion.par, bf16[8,160,128]{2,1,0:T(8,128)(2,1)S(1)} %get-tuple-element.34.own, ...), custom_call_target="tpu_custom_call" | custom-call | flops 1000000 | bytes 2097152 | tf_op jit(solution)/shard_map/pack_x/pallas_call | solution.py:617
  25.9 0.0 copy-start.2
  25.9 0.0 copy-start.3
  25.9 0.0 copy-start.4
  25.9 0.0 copy-start.5
  25.9 0.0 copy-start.6
  25.9 1.3 %collective-permute-start.4 = (bf16[7,160,128]{2,1,0:T(8,128)(2,1)S(1)}, bf16[7,160,128]{2,1,0:T(8,128)(2,1)S(1)}, u32[]{:S(2)}, u32[]{:S(2)}) collective-permute-start(bf16[7,160,128]{2,1,0:T(8,128)(2,1)S(1)} %get-tuple-element.49), channel_id=1, source_target_pairs={{0,4},{4,0},{1,5},{5,1},{2,6},{6,2},{3,7},{7,3},{8,12},{12,8},{9,1... | collective-permute-start | bytes 860168 | tf_op jit(solution)/shard_map/ppermute | solution.py:648
  27.2 0.0 copy-done.1
  27.3 4.1 %rest_operators.1.rest = bf16[112,152,128]{2,1,0:T(8,128)(2,1)S(1)} custom-call(bf16[152,152,316]{2,1,0:T(8,128)(2,1)} %bitcast.6, bf16[316,512]{1,0:T(8,128)(2,1)S(1)} %copy-done.1), custom_call_target="tpu_custom_call" | custom-call | flops 5000000000 | bytes 5242880 | tf_op jit(solution)/shard_map/rest_operators/pallas_call | solution.py:617
  31.4 0.0 copy-done.2
  31.4 0.5 masks.1.keep
  31.9 2.4 %early.1 = (bf16[216,160,128]{2,1,0:T(8,128)(2,1)S(1)}, bf16[49,160,256]{2,1,0:T(8,128)(2,1)S(1)}) custom-call(bf16[8,160,128]{2,1,0:T(8,128)(2,1)S(1)} %get-tuple-element.34.own, bf16[8,160,128]{2,1,0:T(8,128)(2,1)S(1)} %get-tuple-element.47.hz, bf16[8,160,128]{2,1,0:T(8,128)(2,1)S(1)} %get-tuple-element.40.hy, ...), custom_call_target="tpu_custom_call" | custom-call | flops 1000000000 | bytes 8388608 | tf_op jit(solution)/shard_map/early/pallas_call | solution.py:617
  34.4 0.0 collective-permute-done.4.got_a.got_b
  34.4 0.0 copy-done.3
  34.4 0.0 copy-done.4
  34.4 0.0 copy-done.5
  34.4 0.0 copy-done.6
  34.4 20.3 %translate.1 = (bf16[152,1024]{1,0:T(8,128)(2,1)}, bf16[216,160,128]{2,1,0:T(8,128)(2,1)S(1)}, bf16[49,160,256]{2,1,0:T(8,128)(2,1)S(1)}) custom-call(s32[3]{0:T(128)S(1)} %pad_add_fusion.par, bf16[8,160,128]{2,1,0:T(8,128)(2,1)S(1)} %get-tuple-element.34.own, ...), custom_call_target="tpu_custom_call", output_to_operand_aliasing={{1}: (16, {}), {2}: (17, {})} | custom-call | flops 20000000000 | bytes 20971520 | tf_op jit(solution)/shard_map/translate/pallas_call | solution.py:617
Async XLA Ops:
  2.6 8.8 %collective-permute-start = (bf16[3,160,128]{2,1,0:T(8,128)(2,1)S(1)}, bf16[3,160,128]{2,1,0:T(8,128)(2,1)S(1)}, u32[]{:S(2)}, u32[]{:S(2)}) collective-permute-start(bf16[3,160,128]{2,1,0:T(8,128)(2,1)S(1)} %get-tuple-element.36), channel_id=1, source_target_pairs={{0,2},{2,0},{1,3},{3,1},{4,6},{6,4},{5,7},{7,5},{8,10},{10,8},{9,1... | collective-permute-start | bytes 368648 | tf_op jit(solution)/shard_map/ppermute | solution.py:648
  3.9 7.5 %collective-permute-start.1 = (bf16[3,160,128]{2,1,0:T(8,128)(2,1)S(1)}, bf16[3,160,128]{2,1,0:T(8,128)(2,1)S(1)}, u32[]{:S(2)}, u32[]{:S(2)}) collective-permute-start(bf16[3,160,128]{2,1,0:T(8,128)(2,1)S(1)} %get-tuple-element.37), channel_id=1, source_target_pairs={{2,16},{16,2},{3,17},{17,3},{6,20},{20,6},{7,21},{21,7},{10,24},{2... | collective-permute-start | bytes 368648 | tf_op jit(solution)/shard_map/ppermute | solution.py:650
  5.8 5.6 %copy-start = (f32[178,128]{1,0:T(8,128)S(1)}, f32[178,128]{1,0:T(8,128)}, u32[]{:S(2)}) copy-start(f32[178,128]{1,0:T(8,128)} %constant.16.clone.tab_hbm.tab) | copy-start | bytes 273412
  12.5 12.1 %collective-permute-start.2 = (bf16[4,160,128]{2,1,0:T(8,128)(2,1)S(1)}, bf16[4,160,128]{2,1,0:T(8,128)(2,1)S(1)}, u32[]{:S(2)}, u32[]{:S(2)}) collective-permute-start(bf16[4,160,128]{2,1,0:T(8,128)(2,1)S(1)} %get-tuple-element.42), channel_id=1, source_target_pairs={{0,1},{1,0},{2,3},{3,2},{4,5},{5,4},{6,7},{7,6},{8,9},{9,8},{10,11... | collective-permute-start | bytes 491528 | tf_op jit(solution)/shard_map/ppermute | solution.py:648
  14.6 12.7 %copy-start.1 = (bf16[316,512]{1,0:T(8,128)(2,1)S(1)}, bf16[316,512]{1,0:T(8,128)(2,1)}, u32[]{:S(2)}) copy-start(bf16[316,512]{1,0:T(8,128)(2,1)} %constant.17.clone.order) | copy-start | bytes 970756
  14.6 10.0 %collective-permute-start.3 = (bf16[4,160,128]{2,1,0:T(8,128)(2,1)S(1)}, bf16[4,160,128]{2,1,0:T(8,128)(2,1)S(1)}, u32[]{:S(2)}, u32[]{:S(2)}) collective-permute-start(bf16[4,160,128]{2,1,0:T(8,128)(2,1)S(1)} %get-tuple-element.43), channel_id=1, source_target_pairs={{1,8},{8,1},{3,10},{10,3},{5,12},{12,5},{7,14},{14,7},{17,24},{24,... | collective-permute-start | bytes 491528 | tf_op jit(solution)/shard_map/ppermute | solution.py:650
  25.9 5.5 %copy-start.2 = (s32[316,1024]{1,0:T(8,128)S(1)}, s32[316,1024]{1,0:T(8,128)}, u32[]{:S(2)}) copy-start(s32[316,1024]{1,0:T(8,128)} %fine.1) | copy-start | bytes 3883012
  25.9 8.5 %copy-start.3 = (bf16[8,152,152]{2,1,0:T(8,128)(2,1)S(1)}, bf16[8,152,152]{2,1,0:T(8,128)(2,1)}, u32[]{:S(2)}) copy-start(bf16[8,152,152]{2,1,0:T(8,128)(2,1)} %down.1) | copy-start | bytes 1108996
  25.9 8.5 %copy-start.4 = (s32[316,128]{1,0:T(8,128)S(1)}, s32[316,128]{1,0:T(8,128)}, u32[]{:S(2)}) copy-start(s32[316,128]{1,0:T(8,128)} %clist.1) | copy-start | bytes 485380
  25.9 8.5 %copy-start.5 = (bf16[152,152]{1,0:T(8,128)(2,1)S(1)}, bf16[152,152]{1,0:T(8,128)(2,1)}, u32[]{:S(2)}) copy-start(bf16[152,152]{1,0:T(8,128)(2,1)} %inverse.1) | copy-start | bytes 138628
  25.9 8.5 %copy-start.6 = (f32[320,128]{1,0:T(8,128)S(1)}, f32[320,128]{1,0:T(8,128)}, u32[]{:S(2)}) copy-start(f32[320,128]{1,0:T(8,128)} %constant.18.clone.outside) | copy-start | bytes 491524
  25.9 8.4 %collective-permute-start.4 = (bf16[7,160,128]{2,1,0:T(8,128)(2,1)S(1)}, bf16[7,160,128]{2,1,0:T(8,128)(2,1)S(1)}, u32[]{:S(2)}, u32[]{:S(2)}) collective-permute-start(bf16[7,160,128]{2,1,0:T(8,128)(2,1)S(1)} %get-tuple-element.49), channel_id=1, source_target_pairs={{0,4},{4,0},{1,5},{5,1},{2,6},{6,2},{3,7},{7,3},{8,12},{12,8},{9,1... | collective-permute-start | bytes 860168 | tf_op jit(solution)/shard_map/ppermute | solution.py:648
